TPU v7x, 512 devices: a whole 4x4x16 slice. The times are simulated.
512 devices in a mesh: grp: 8 (over x, y_lo), par: 64 (over z, y_hi, core).
Axes of the slice: x: 4, y: 4 (y_hi: 2, y_lo: 2; y = y_hi * 2 + y_lo), z: 16, core: 2. Of those that a mesh axis runs over, the one named last changes fastest.
Arguments:
- omega: bfloat16 [32, 524288], P(None, 'par'), may hold values from -6 to 6
- jac_blocks: bfloat16 [8, 8192, 128, 128], P('grp', 'par'), may hold values from -0.1796875 to 0.1796875
- block_param: int32 [8, 8192], P('grp', 'par'), may hold values from 0 to 63
- block_obs: int32 [8, 8192], P('grp', 'par'), may hold values from 0 to 63
- block_count: int32 [8, 64], P('grp', 'par'), may hold values from 16 to 128, as said below
- obs_weight: float32 [8, 8192], P('grp'), may hold values from 0.1 to 1
Outputs:
- hess_probe: float32 [32, 524288], P(None, ('par', 'grp'))
Inputs may be any that keep to these rules, and one draw needn't show every extreme that they name: `block_count`: in every group four devices use all 128 slots and one device uses the fewest; the others use at most 64.
All inputs are finite; a program needn't handle non-finite values.
Results may differ from a plain program's by a relative error of at most 0.0027.
Values may be sent and summed in bfloat16 or wider, within the bound.
No kernel may reach another device: no remote copies, remote signals or barrier semaphores. Data moves between devices by JAX's collectives and lax.ppermute only.
A program may use at most 64 MiB of HBM per device.

v0:
```python
import jax
import jax.numpy as jnp
from jax import lax
from jax.sharding import PartitionSpec as P


def on_device(omega, jac_blocks, block_param, block_obs, block_count, obs_weight):
    probes = omega.shape[0]
    width = jac_blocks.shape[2]
    slots = jac_blocks.shape[1]
    pblocks = omega.shape[1] // width
    oblocks = obs_weight.shape[1] // width
    blocks = jac_blocks[0]
    bparam = block_param[0]
    bobs = block_obs[0]
    weights = obs_weight[0]
    active = (jnp.arange(slots, dtype=jnp.int32) < block_count[0, 0]).astype(jnp.float32)
    panels = omega.reshape(probes, pblocks, width)
    picked = jnp.take(panels, bparam, axis=1)
    terms = jnp.einsum("kcp,cpo->cko", picked, blocks, preferred_element_type=jnp.float32)
    terms = terms * active[:, None, None]
    partial_value = jax.ops.segment_sum(terms, bobs, num_segments=oblocks)
    partial_value = jnp.transpose(partial_value, (1, 0, 2)).reshape(probes, oblocks * width)
    fwd = lax.psum(partial_value, "par")
    scaled = (fwd * weights[None, :]).astype(jnp.bfloat16)
    vblocks = scaled.reshape(probes, oblocks, width)
    pickv = jnp.take(vblocks, bobs, axis=1)
    back = jnp.einsum("kco,cpo->ckp", pickv, blocks, preferred_element_type=jnp.float32)
    back = back * active[:, None, None]
    local_terms = jax.ops.segment_sum(back, bparam, num_segments=pblocks)
    local_terms = jnp.transpose(local_terms, (1, 0, 2)).reshape(probes, pblocks * width)
    return lax.psum_scatter(local_terms, "grp", scatter_dimension=1, tiled=True)


def solution(mesh):
    in_specs = (
        P(None, "par"),
        P("grp", "par", None, None),
        P("grp", "par"),
        P("grp", "par"),
        P("grp", "par"),
        P("grp", None),
    )
    out_specs = P(None, ("par", "grp"))
    return jax.shard_map(
        on_device, mesh=mesh, in_specs=in_specs, out_specs=out_specs, check_vma=False
    )
```

profile of v0, /device:TPU:1, one launch (start us, length us, event | category | flops | bytes accessed | tf_op | source)
XLA Modules:
  0.0 630.5 jit_solution(9060553910922731340)
XLA Ops:
  6.5 0.0 copy-start
  6.5 0.0 all-reduce.2.cloned.1.call-start
  7.2 0.7 compare_select_fusion.1
  7.9 0.7 compare_and_fusion.1
  8.6 0.0 copy-done
  8.6 0.1 copy_bitcast_fusion.3
  8.7 0.8 gather_fusion
  9.4 0.0 copy-start.3
  9.5 4.8 fusion.4
  14.3 0.1 broadcast.10.clone
  14.4 0.0 copy-done.3
  14.4 11.7 %scatter_fusion = f32[64,32,128]{2,1,0:T(8,128)S(1)} fusion(f32[64,32,128]{2,1,0:T(8,128)S(1)} %broadcast.10.clone, s32[128]{0:T(128)S(1)} %bitcast.50, f32[128,32,128]{2,1,0:T(8,128)} %fusion.4), kind=kCustom, calls=%fused_computation.2 | custom fusion | flops 524288 | bytes 6291968 | tf_op jit(solution)/shard_map/scatter-add | solution.py:22
  26.1 0.0 copy-start.1
  26.1 1.1 copy_bitcast_fusion.1
  27.2 0.0 all-reduce.2.cloned.1.call-update
  27.2 0.0 reduce-scatter.2.cloned.1.call-start
  27.3 533.9 %all-reduce.2.cloned.1.call-done = f32[32,8192]{1,0:T(8,128)} async-done(((f32[32,8192]{1,0:T(8,128)}), f32[32,8192]{1,0:T(8,128)}) %all-reduce.2.cloned.1.call-update) | async-done | bytes 1048592 | tf_op jit(solution)/shard_map/psum | solution.py:24
  561.2 0.0 copy-done.1
  561.2 1.3 copy_bitcast_fusion.2
  562.5 0.8 gather_fusion.1
  563.3 0.0 copy-start.2
  563.3 5.9 fusion.7
  569.2 0.1 broadcast.10
  569.3 0.0 copy-done.2
  569.3 11.7 %scatter_fusion.1 = f32[64,32,128]{2,1,0:T(8,128)S(1)} fusion(f32[64,32,128]{2,1,0:T(8,128)S(1)} %broadcast.10, s32[128]{0:T(128)S(1)} %bitcast.49, f32[128,32,128]{2,1,0:T(8,128)} %fusion.7), kind=kCustom, calls=%fused_computation.3 | custom fusion | flops 524288 | bytes 6291968 | tf_op jit(solution)/shard_map/scatter-add | solution.py:30
  581.0 1.1 copy_bitcast_fusion
  582.1 0.0 reduce-scatter.2.cloned.1.call-update
  582.1 41.6 %reduce-scatter.2.cloned.1.call-done = f32[32,1024]{1,0:T(8,128)} async-done(((f32[32,8192]{1,0:T(8,128)}), f32[32,1024]{1,0:T(8,128)}) %reduce-scatter.2.cloned.1.call-update) | async-done | bytes 131088 | tf_op jit(solution)/shard_map/reduce_scatter | solution.py:32
  (4 shorter events, 0.0 us)
Async XLA Ops:
  6.5 2.0 copy-start
  6.5 554.7 %all-reduce.2.cloned.1.call-start = ((), (), s32[]{:S(2)}) async-start(), calls=%async_computation.1 | async-start | bytes 2097152 | tf_op jit(solution)/shard_map/psum | solution.py:24
  9.4 4.9 copy-start.3
  26.1 535.1 %copy-start.1 = (f32[1,8192]{1,0:T(1,128)S(1)}, f32[1,8192]{1,0:T(1,128)}, u32[]{:S(2)}) copy-start(f32[1,8192]{1,0:T(1,128)} %param.13) | copy-start | bytes 98308
  27.2 596.4 %reduce-scatter.2.cloned.1.call-start = ((), (), s32[]{:S(2)}) async-start(), calls=%async_computation.2 | async-start | bytes 1179648 | tf_op jit(solution)/shard_map/reduce_scatter | solution.py:32
  563.3 6.0 copy-start.2
Sparse Core Ops, SparseCore 0:
  27.4 533.7 all-reduce.1
  582.2 41.3 reduce-scatter.1
where the time goes:
time: 635 us; the launch traced here: 630 us
  waiting for transfers between devices  575 us (91%)
  other arithmetic  26 us (4%)
  between operations  14.2 us (2%)
  matrix products  10.7 us (2%)
    psum x1, waiting for transfers between devices, on_device(): fwd = lax.psum(partial_value, 'par')  534 us
    reduce_scatter x1, waiting for transfers between devices, on_device(): return lax.psum_scatter(local_terms, 'grp', scatter_dimension=1, tiled=True)  41.6 us
  transfers between devices with their start and end apart: 2, of which 2 were waited for; matrix products, arithmetic and copies ran while one was open for 0% of the time, Pallas kernels for 0%

commit v1 on v0

v1 whole, which is shorter than its diff:
```python
import jax
import jax.numpy as jnp
from jax import lax
from jax.experimental import pallas as pl
from jax.experimental.pallas import tpu as pltpu
from jax.sharding import Mesh, PartitionSpec as P

CHUNK = 16
PAR = ("z", "yh", "core")
GRP = ("x", "yl")


def fetch(n, jac_hbm, buf, sems):
    def copy(c):
        at = pl.ds(pl.multiple_of(c * CHUNK, CHUNK), CHUNK)
        return pltpu.make_async_copy(jac_hbm.at[0, at], buf.at[at], sems.at[c])

    for c in range(buf.shape[0] // CHUNK):

        @pl.when(c * CHUNK < n)
        def _():
            copy(c).start()

    return copy


def fwd_kernel(cnt_ref, bp_ref, bo_ref, omega_ref, jac_hbm, out_ref, buf, sems):
    width = buf.shape[1]
    n = cnt_ref[0, 0]
    copy = fetch(n, jac_hbm, buf, sems)
    out_ref[...] = jnp.zeros_like(out_ref)

    def step(c, carry):
        copy(c).wait()
        for j in range(CHUNK):
            s = c * CHUNK + j
            at = pl.multiple_of(bp_ref[0, s] * width, width)
            panel = omega_ref[:, pl.ds(at, width)]
            panel = jnp.where(s < n, panel, jnp.zeros_like(panel))
            term = jnp.dot(panel, buf[s], preferred_element_type=jnp.float32)
            o = bo_ref[0, s]
            out_ref[o] = out_ref[o] + term
        return carry

    lax.fori_loop(0, (n + CHUNK - 1) // CHUNK, step, 0)


def bwd_kernel(cnt_ref, bp_ref, bo_ref, v_ref, jac_hbm, out_ref, acc, buf, sems):
    n = cnt_ref[0, 0]
    copy = fetch(n, jac_hbm, buf, sems)
    acc[...] = jnp.zeros_like(acc)

    def step(c, carry):
        copy(c).wait()
        for j in range(CHUNK):
            s = c * CHUNK + j
            v = v_ref[bo_ref[0, s]]
            v = jnp.where(s < n, v, jnp.zeros_like(v))
            term = lax.dot_general(
                v, buf[s], (((1,), (1,)), ((), ())), preferred_element_type=jnp.float32
            )
            p = bp_ref[0, s]
            acc[p] = acc[p] + term
        return carry

    lax.fori_loop(0, (n + CHUNK - 1) // CHUNK, step, 0)
    out_ref[...] = acc[...].astype(out_ref.dtype)


def on_device(omega, jac_blocks, block_param, block_obs, block_count, obs_weight):
    probes = omega.shape[0]
    slots, width = jac_blocks.shape[1], jac_blocks.shape[2]
    pblocks = omega.shape[1] // width
    oblocks = obs_weight.shape[1] // width
    smem = pl.BlockSpec(memory_space=pltpu.SMEM)
    vmem = pl.BlockSpec(memory_space=pltpu.VMEM)
    hbm = pl.BlockSpec(memory_space=pltpu.HBM)
    blocks = pltpu.VMEM((slots, width, width), jac_blocks.dtype)
    done = pltpu.SemaphoreType.DMA((slots // CHUNK,))
    params = pltpu.CompilerParams(vmem_limit_bytes=24 << 20)

    partial_sum = pl.pallas_call(
        fwd_kernel,
        out_shape=jax.ShapeDtypeStruct((oblocks, probes, width), jnp.float32),
        in_specs=[smem, smem, smem, vmem, hbm],
        out_specs=vmem,
        scratch_shapes=[blocks, done],
        compiler_params=params,
        name="fwd_blocks",
    )(block_count, block_param, block_obs, omega, jac_blocks)

    def swap_sum(v, axes):
        n = lax.axis_size(axes)
        v = lax.all_to_all(v, axes, 0, 0, tiled=True)
        return jnp.sum(v.reshape(n, v.shape[0] // n, probes, width), axis=0)

    owned = swap_sum(partial_sum, "core")
    owned = swap_sum(owned, "yh")
    owned = swap_sum(owned, "z")
    mine = (lax.axis_index("core") * 2 + lax.axis_index("yh")) * 16 + lax.axis_index("z")
    weight = lax.dynamic_slice(obs_weight.reshape(oblocks, 1, width), (mine, 0, 0), (1, 1, width))
    scaled = (owned * weight).astype(jnp.bfloat16)
    nz = lax.axis_size("z")
    scaled = lax.all_to_all(jnp.broadcast_to(scaled, (nz, probes, width)), "z", 0, 0, tiled=True)
    scaled = lax.all_gather(scaled, "yh", axis=0, tiled=True)
    scaled = lax.all_gather(scaled, "core", axis=0, tiled=True)

    local_terms = pl.pallas_call(
        bwd_kernel,
        out_shape=jax.ShapeDtypeStruct((pblocks, probes, width), jnp.bfloat16),
        in_specs=[smem, smem, smem, vmem, hbm],
        out_specs=vmem,
        scratch_shapes=[pltpu.VMEM((pblocks, probes, width), jnp.float32), blocks, done],
        compiler_params=params,
        name="bwd_blocks",
    )(block_count, block_param, block_obs, scaled, jac_blocks)

    n = lax.axis_size(GRP)
    got = lax.all_to_all(local_terms, GRP, 0, 0, tiled=True)
    got = got.reshape(n, pblocks // n, probes, width).astype(jnp.float32)
    total = jnp.sum(got, axis=0)
    return jnp.transpose(total, (1, 0, 2)).reshape(probes, pblocks // n * width)


def solution(mesh):
    mesh = Mesh(mesh.devices.reshape(4, 2, 16, 2, 2), GRP + PAR)
    in_specs = (
        P(None, PAR),
        P(GRP, PAR, None, None),
        P(GRP, PAR),
        P(GRP, PAR),
        P(GRP, PAR),
        P(GRP, None),
    )
    out_specs = P(None, PAR + GRP)
    return jax.shard_map(
        on_device, mesh=mesh, in_specs=in_specs, out_specs=out_specs, check_vma=False
    )
```

time: 635 us -> 109 us (0.17)
  waiting for transfers between devices: 575 us -> 12.7 us
  blocking collectives: 0 us -> 69.5 us
  other arithmetic: 26 us -> 0.94 us
  between operations: 14.2 us -> 0.76 us
  matrix products: 10.7 us -> 0 us
  starting transfers between devices: 0.04 us -> 9.61 us
  Pallas kernels: 0 us -> 7.26 us
    psum x1 -> x0, waiting for transfers between devices: 534 us -> none  [on_device(): fwd = lax.psum(partial_value, 'par')]
    all_to_all x0 -> x4, blocking collectives: none -> 56.9 us  [the longest x2 22.7 us: swap_sum(): v = lax.all_to_all(v, axes, 0, 0, tiled=True)]
    reduce_scatter x1 -> x0, waiting for transfers between devices: 41.6 us -> none  [on_device(): return lax.psum_scatter(local_terms, 'grp', scatter_dimension=1, tiled=True)]
    scatter-add x2 -> x0, other arithmetic: 23.4 us -> none  [the longest x1 11.7 us: on_device(): partial_value = jax.ops.segment_sum(terms, bobs, num_segments=oblocks)]
    all_to_all x0 -> x1, waiting for transfers between devices: none -> 12.7 us  [swap_sum(): v = lax.all_to_all(v, axes, 0, 0, tiled=True)]
    all_gather x0 -> x2, blocking collectives: none -> 12.5 us  [the longest x1 6.54 us: on_device(): scaled = lax.all_gather(scaled, 'core', axis=0, tiled=True)]
    dot_general x2 -> x0, matrix products: 10.7 us -> none  [the longest x1 5.88 us: on_device(): jnp.einsum('kco,cpo->ckp', pickv, blocks, preferred_element_type=jnp.floa...]
    all_to_all x0 -> x1, starting transfers between devices: none -> 9.61 us  [swap_sum(): v = lax.all_to_all(v, axes, 0, 0, tiled=True)]
  transfers between devices with their start and end apart: 2 -> 1, of which waited for: 2 -> 1; matrix products, arithmetic and copies ran while one was open for 0% -> 0% of each run, Pallas kernels for 0% -> 0%
where the time goes in v1:
time: 109 us; the launch traced here: 108 us
  blocking collectives  69.5 us (64%)
  waiting for transfers between devices  12.7 us (12%)
  starting transfers between devices  9.61 us (9%)
  local copies, waits for them, and re-layouts  7.43 us (7%)
  Pallas kernels  7.26 us (7%)
    all_to_all x2, blocking collectives, swap_sum(): v = lax.all_to_all(v, axes, 0, 0, tiled=True)  22.7 us
    all_to_all x1, blocking collectives, on_device(): lax.all_to_all(jnp.broadcast_to(scaled, (nz, probes, width)), 'z', 0, 0,...  22.5 us
    all_to_all x1, waiting for transfers between devices, swap_sum(): v = lax.all_to_all(v, axes, 0, 0, tiled=True)  12.7 us
    all_to_all x1, blocking collectives, on_device(): got = lax.all_to_all(local_terms, GRP, 0, 0, tiled=True)  11.8 us
    all_to_all x1, starting transfers between devices, swap_sum(): v = lax.all_to_all(v, axes, 0, 0, tiled=True)  9.61 us
    unnamed x16, local copies, waits for them, and re-layouts  6.74 us
    all_gather x1, blocking collectives, on_device(): scaled = lax.all_gather(scaled, 'core', axis=0, tiled=True)  6.54 us
    all_gather x1, blocking collectives, on_device(): scaled = lax.all_gather(scaled, 'yh', axis=0, tiled=True)  5.99 us
  transfers between devices with their start and end apart: 1, of which 1 were waited for; matrix products, arithmetic and copies ran while one was open for 0% of the time, Pallas kernels for 0%

profile of v1, /device:TPU:1, one launch (start us, length us, event | category | flops | bytes accessed | tf_op | source)
XLA Modules:
  0.0 108.2 jit_solution(17728196109440332923)
XLA Ops:
  0.0 0.0 copy-start
  0.7 0.0 copy-start.1
  0.7 2.2 %copy-done.1 = bf16[1,128,128,128]{3,2,1,0:T(8,128)(2,1)S(1)} copy-done((bf16[1,128,128,128]{3,2,1,0:T(8,128)(2,1)S(1)}, bf16[1,128,128,128]{3,2,1,0:T(8,128)(2,1)}, u32[]{:S(2)}) %copy-start.1) | copy-done | bytes 4194328
  2.9 0.0 copy-start.3
  2.9 1.0 copy-done.3
  3.9 0.0 copy-start.4
  3.9 0.7 copy-done.4
  4.6 0.0 copy-start.6
  4.6 0.7 copy-done.6
  5.2 3.1 %fwd_blocks.1 = f32[64,32,128]{2,1,0:T(8,128)S(1)} custom-call(s32[1,1]{1,0:T(1,128)S(6)} %copy.15.cnt_ref, s32[1,128]{1,0:T(1,128)S(1)} %copy-done.4, s32[1,128]{1,0:T(1,128)S(1)} %copy-done.6, bf16[32,8192]{1,0:T(8,128)(2,1)S(1)} %copy-done.3, bf16[1,128,128,128]{3,2,1,0:T(8,128)(2,1)S(1)} %copy-done.1), custom_call_target="tpu_custom_call" | custom-call | tf_op jit(solution)/shard_map/fwd_blocks/pallas_call | solution.py:82
  8.3 0.0 copy-start.5
  8.3 0.0 copy-start.7
  8.3 11.1 %all_to_all.25 = f32[64,32,128]{2,1,0:T(8,128)S(1)} all-to-all(f32[64,32,128]{2,1,0:T(8,128)S(1)} %fwd_blocks.1), channel_id=1, replica_groups=mesh['x'=4,'yl'=2,'z'=16,'yh'=2,'core'=2] {'core'}, dimensions={0} | all-to-all | bytes 2097152 | tf_op jit(solution)/shard_map/all_to_all | solution.py:94
  19.4 0.1 reduce_sum.36
  19.5 11.6 %all_to_all.26 = f32[32,32,128]{2,1,0:T(8,128)S(1)} all-to-all(f32[32,32,128]{2,1,0:T(8,128)S(1)} %reduce_sum.36), channel_id=1, replica_groups=mesh['x'=4,'yl'=2,'z'=16,'yh'=2,'core'=2] {'yh'}, dimensions={0} | all-to-all | bytes 1048576 | tf_op jit(solution)/shard_map/all_to_all | solution.py:94
  31.2 0.7 reduce_sum.37
  31.9 9.6 %all-to-all-start.2 = ((f32[16,32,128]{2,1,0:T(8,128)}), f32[16,32,128]{2,1,0:T(8,128)S(1)}, u32[]{:S(2)}, u32[]{:S(2)}) async-start(f32[16,32,128]{2,1,0:T(8,128)} %reduce_sum.37), calls=%async_computation.2 | async-start | bytes 524288 | tf_op jit(solution)/shard_map/all_to_all | solution.py:94
  41.5 0.0 copy-done
  41.5 12.7 %all-to-all-done.2 = f32[16,32,128]{2,1,0:T(8,128)S(1)} async-done(((f32[16,32,128]{2,1,0:T(8,128)}), f32[16,32,128]{2,1,0:T(8,128)S(1)}, u32[]{:S(2)}, u32[]{:S(2)}) %all-to-all-start.2) | async-done | bytes 262176 | tf_op jit(solution)/shard_map/all_to_all | solution.py:94
  54.4 22.5 %all_to_all.27 = bf16[16,32,128]{2,1,0:T(8,128)(2,1)S(1)} all-to-all(bf16[16,32,128]{2,1,0:T(8,128)(2,1)S(1)} %broadcast_in_dim.2), channel_id=1, replica_groups=mesh['x'=4,'yl'=2,'z'=16,'yh'=2,'core'=2] {'z'}, dimensions={0} | all-to-all | bytes 262144 | tf_op jit(solution)/shard_map/all_to_all | solution.py:104
  76.8 6.0 %all_gather.6 = bf16[32,32,128]{2,1,0:T(8,128)(2,1)S(1)} all-gather(bf16[16,32,128]{2,1,0:T(8,128)(2,1)S(1)} %all_to_all.27), channel_id=1, replica_groups=mesh['x'=4,'yl'=2,'z'=16,'yh'=2,'core'=2] {'yh'}, dimensions={0}, use_global_device_ids=true | all-gather | bytes 393216 | tf_op jit(solution)/shard_map/all_gather | solution.py:105
  82.8 6.5 %all_gather.7.v_ref = bf16[64,32,128]{2,1,0:T(8,128)(2,1)S(1)} all-gather(bf16[32,32,128]{2,1,0:T(8,128)(2,1)S(1)} %all_gather.6), channel_id=1, replica_groups=mesh['x'=4,'yl'=2,'z'=16,'yh'=2,'core'=2] {'core'}, dimensions={0}, use_global_device_ids=true | all-gather | bytes 786432 | tf_op jit(solution)/shard_map/all_gather | solution.py:106
  89.3 0.0 copy-done.5
  89.3 0.0 copy-done.7
  89.3 0.0 copy-start.2
  89.3 2.2 %copy-done.2 = bf16[1,128,128,128]{3,2,1,0:T(8,128)(2,1)S(1)} copy-done((bf16[1,128,128,128]{3,2,1,0:T(8,128)(2,1)S(1)}, bf16[1,128,128,128]{3,2,1,0:T(8,128)(2,1)}, u32[]{:S(2)}) %copy-start.2) | copy-done | bytes 4194328
  91.5 4.2 %bwd_blocks.1 = bf16[64,32,128]{2,1,0:T(8,128)(2,1)S(1)} custom-call(s32[1,1]{1,0:T(1,128)S(6)} %copy.15.cnt_ref, s32[1,128]{1,0:T(1,128)S(1)} %copy-done.5, s32[1,128]{1,0:T(1,128)S(1)} %copy-done.7, bf16[64,32,128]{2,1,0:T(8,128)(2,1)S(1)} %all_gather.7.v_ref, bf16[1,128,128,128]{3,2,1,0:T(8,128)(2,1)S(1)} %copy-done.2), custom_call_target="tpu_custom_call" | custom-call | tf_op jit(solution)/shard_map/bwd_blocks/pallas_call | solution.py:108
  95.7 11.8 %all_to_all.28 = bf16[64,32,128]{2,1,0:T(8,128)(2,1)S(1)} all-to-all(bf16[64,32,128]{2,1,0:T(8,128)(2,1)S(1)} %bwd_blocks.1), channel_id=1, replica_groups=mesh['x'=4,'yl'=2,'z'=16,'yh'=2,'core'=2] {'x','yl'}, dimensions={0} | all-to-all | bytes 1048576 | tf_op jit(solution)/shard_map/all_to_all | solution.py:119
  107.5 0.1 convert_reduce_fusion
  107.5 0.7 copy_bitcast_fusion
  (4 shorter events, 0.1 us)
Async XLA Ops:
  0.0 41.5 %copy-start = (f32[1,8192]{1,0:T(1,128)S(1)}, f32[1,8192]{1,0:T(1,128)}, u32[]{:S(2)}) copy-start(f32[1,8192]{1,0:T(1,128)} %param.11) | copy-start | bytes 98308
  0.7 2.2 %copy-start.1 = (bf16[1,128,128,128]{3,2,1,0:T(8,128)(2,1)S(1)}, bf16[1,128,128,128]{3,2,1,0:T(8,128)(2,1)}, u32[]{:S(2)}) copy-start(bf16[1,128,128,128]{3,2,1,0:T(8,128)(2,1)} %jac_hbm.3) | copy-start | bytes 12582916
  2.9 1.0 copy-start.3
  3.9 0.7 copy-start.4
  4.6 0.7 copy-start.6
  8.3 81.0 %copy-start.5 = (s32[1,128]{1,0:T(1,128)S(1)}, s32[1,128]{1,0:T(1,128)}, u32[]{:S(2)}) copy-start(s32[1,128]{1,0:T(1,128)} %bp_ref.3) | copy-start | bytes 1540
  8.3 81.0 %copy-start.7 = (s32[1,128]{1,0:T(1,128)S(1)}, s32[1,128]{1,0:T(1,128)}, u32[]{:S(2)}) copy-start(s32[1,128]{1,0:T(1,128)} %bo_ref.3) | copy-start | bytes 1540
  31.9 22.4 %all-to-all-start.2 = ((f32[16,32,128]{2,1,0:T(8,128)}), f32[16,32,128]{2,1,0:T(8,128)S(1)}, u32[]{:S(2)}, u32[]{:S(2)}) async-start(f32[16,32,128]{2,1,0:T(8,128)} %reduce_sum.37), calls=%async_computation.2 | async-start | bytes 524288 | tf_op jit(solution)/shard_map/all_to_all | solution.py:94
  89.3 2.2 %copy-start.2 = (bf16[1,128,128,128]{3,2,1,0:T(8,128)(2,1)S(1)}, bf16[1,128,128,128]{3,2,1,0:T(8,128)(2,1)}, u32[]{:S(2)}) copy-start(bf16[1,128,128,128]{3,2,1,0:T(8,128)(2,1)} %jac_hbm.3) | copy-start | bytes 12582916

commit v2 on v1

v2 whole, which is shorter than its diff:
```python
import jax
import jax.numpy as jnp
from jax import lax
from jax.experimental import pallas as pl
from jax.experimental.pallas import tpu as pltpu
from jax.sharding import Mesh, PartitionSpec as P

CHUNK = 16
SUB = 8
PAR = ("z", "yh", "core")
GRP = ("x", "yl")


def fetch(n, jac_hbm, jac, sems):
    def chunk(c):
        at = pl.ds(pl.multiple_of(c * CHUNK, CHUNK), CHUNK)
        return pltpu.make_async_copy(jac_hbm.at[0, at], jac.at[at], sems.at[c])

    for c in range(jac.shape[0] // CHUNK):

        @pl.when(c * CHUNK < n)
        def _():
            chunk(c).start()

    return chunk


def fwd_kernel(cnt, bp_hbm, bo_hbm, omega_hbm, jac_hbm, out_ref, bp, bo, jac, omega, sems, jsems):
    width = jac.shape[1]
    probes = omega.shape[0]
    half = (out_ref.shape[1] - SUB) // probes
    small = [
        pltpu.make_async_copy(src, dst, sems.at[i])
        for i, (src, dst) in enumerate(((bp_hbm, bp), (bo_hbm, bo), (omega_hbm, omega)))
    ]
    for copy in small:
        copy.start()

    n = cnt[0, 0]
    chunk = fetch(n, jac_hbm, jac, jsems)
    out_ref[...] = jnp.zeros_like(out_ref)
    for copy in small:
        copy.wait()

    def step(c, carry):
        chunk(c).wait()
        for j in range(CHUNK):
            s = c * CHUNK + j
            at = pl.multiple_of(bp[0, s] * width, width)
            panel = omega[:, pl.ds(at, width)]
            panel = jnp.where(s < n, panel, jnp.zeros_like(panel))
            term = jnp.dot(panel, jac[s], preferred_element_type=jnp.float32)
            o = bo[0, s]
            rows = pl.ds(pl.multiple_of((o % half) * probes, probes), probes)
            out_ref[o // half, rows] = out_ref[o // half, rows] + term
        return carry

    lax.fori_loop(0, (n + CHUNK - 1) // CHUNK, step, 0)
    body = out_ref.shape[1] - SUB
    top = jnp.zeros((SUB, width), jnp.float32)
    for i in range(2):
        top = jnp.maximum(top, jnp.max(jnp.abs(out_ref[i, :body].reshape(body // SUB, SUB, width)), axis=0))
    for i in range(2):
        out_ref[i, body:] = top


def pack_kernel(pair_ref, out_ref):
    rows = pair_ref.shape[1] - SUB
    parts, each, width = out_ref.shape
    each = each - SUB
    top = pair_ref[0, rows:] + pair_ref[1, rows:]
    power = jnp.clip(jnp.ceil(jnp.log2(top)), -100.0, 100.0) - 14.0
    data = pair_ref[0, :rows] + pair_ref[1, :rows]
    data = data.reshape(rows // SUB, SUB, width) * jnp.exp2(-power)
    out_ref[:, :each] = data.reshape(parts, each, width)
    out_ref[:, each:] = jnp.broadcast_to(power, (parts, SUB, width))


def bwd_kernel(cnt_ref, bp_ref, bo_ref, v_ref, jac_hbm, out_ref, acc, jac_ref, jsems):
    n = cnt_ref[0, 0]
    chunk = fetch(n, jac_hbm, jac_ref, jsems)
    acc[...] = jnp.zeros_like(acc)

    def step(c, carry):
        chunk(c).wait()
        for j in range(CHUNK):
            s = c * CHUNK + j
            v = v_ref[bo_ref[0, s]]
            v = jnp.where(s < n, v, jnp.zeros_like(v))
            term = lax.dot_general(
                v, jac_ref[s], (((1,), (1,)), ((), ())), preferred_element_type=jnp.float32
            )
            p = bp_ref[0, s]
            acc[p] = acc[p] + term
        return carry

    lax.fori_loop(0, (n + CHUNK - 1) // CHUNK, step, 0)
    out_ref[...] = acc[...].astype(out_ref.dtype)


def on_device(omega, jac_blocks, block_param, block_obs, block_count, obs_weight):
    probes = omega.shape[0]
    slots, width = jac_blocks.shape[1], jac_blocks.shape[2]
    pblocks = omega.shape[1] // width
    oblocks = obs_weight.shape[1] // width
    nz, nyh, ncore = (lax.axis_size(a) for a in PAR)
    smem = pl.BlockSpec(memory_space=pltpu.SMEM)
    vmem = pl.BlockSpec(memory_space=pltpu.VMEM)
    hbm = pl.BlockSpec(memory_space=pltpu.HBM)
    params = pltpu.CompilerParams(vmem_limit_bytes=24 << 20)
    blocks = pltpu.VMEM((slots, width, width), jac_blocks.dtype)
    done = pltpu.SemaphoreType.DMA((slots // CHUNK,))
    held = [
        pltpu.with_memory_space_constraint(a, pltpu.HBM)
        for a in (block_param, block_obs, omega, jac_blocks)
    ]
    rows = oblocks // ncore * probes
    partial_sum, bp, bo = pl.pallas_call(
        fwd_kernel,
        out_shape=(
            jax.ShapeDtypeStruct((ncore, rows + SUB, width), jnp.float32),
            jax.ShapeDtypeStruct(block_param.shape, jnp.int32),
            jax.ShapeDtypeStruct(block_obs.shape, jnp.int32),
        ),
        in_specs=[smem] + [hbm] * 4,
        out_specs=(vmem, smem, smem),
        scratch_shapes=[
            blocks,
            pltpu.VMEM(omega.shape, omega.dtype),
            pltpu.SemaphoreType.DMA((3,)),
            done,
        ],
        compiler_params=params,
        name="fwd_blocks",
    )(block_count, *held)

    each = rows // nz
    per = each // probes
    first = (lax.axis_index("core") * nz + lax.axis_index("z")) * per
    weight = lax.dynamic_slice(obs_weight.reshape(oblocks, 1, width), (first, 0, 0), (per, 1, width))
    partial_sum, weight = lax.optimization_barrier((partial_sum, weight))
    pair = lax.all_to_all(partial_sum, "core", 0, 0, tiled=True)
    packed = pl.pallas_call(
        pack_kernel,
        out_shape=jax.ShapeDtypeStruct((nz, each + SUB, width), jnp.float32),
        in_specs=[vmem],
        out_specs=vmem,
        compiler_params=pltpu.CompilerParams(vmem_limit_bytes=8 << 20),
        name="pair_sum_scaled",
    )(pair)
    got = lax.all_to_all(packed.astype(jnp.float16), "z", 0, 0, tiled=True)
    scale = jnp.exp2(got[:, each:].astype(jnp.float32))
    data = got[:, :each].astype(jnp.float32).reshape(nz, each // SUB, SUB, width)
    owned = jnp.sum(data * scale[:, None], axis=0).reshape(each // probes, probes, width)
    owned = owned + lax.ppermute(owned, "yh", [(i, nyh - 1 - i) for i in range(nyh)])

    scaled = (owned * weight).astype(jnp.bfloat16)
    scaled = jnp.broadcast_to(scaled, (nz, per, probes, width)).reshape(nz * per, probes, width)
    scaled = lax.all_to_all(scaled, "z", 0, 0, tiled=True)
    scaled = lax.all_gather(scaled, "core", axis=0, tiled=True)

    local_terms = pl.pallas_call(
        bwd_kernel,
        out_shape=jax.ShapeDtypeStruct((pblocks, probes, width), jnp.bfloat16),
        in_specs=[smem, smem, smem, vmem, hbm],
        out_specs=vmem,
        scratch_shapes=[pltpu.VMEM((pblocks, probes, width), jnp.float32), blocks, done],
        compiler_params=params,
        name="bwd_blocks",
    )(block_count, bp, bo, scaled, held[3])

    n = lax.axis_size(GRP)
    got = lax.all_to_all(local_terms, GRP, 0, 0, tiled=True)
    got = got.reshape(n, pblocks // n, probes, width).astype(jnp.float32)
    total = jnp.sum(got, axis=0)
    return jnp.transpose(total, (1, 0, 2)).reshape(probes, pblocks // n * width)


def solution(mesh):
    mesh = Mesh(mesh.devices.reshape(4, 2, 16, 2, 2), GRP + PAR)
    in_specs = (
        P(None, PAR),
        P(GRP, PAR, None, None),
        P(GRP, PAR),
        P(GRP, PAR),
        P(GRP, PAR),
        P(GRP, None),
    )
    out_specs = P(None, PAR + GRP)
    return jax.shard_map(
        on_device, mesh=mesh, in_specs=in_specs, out_specs=out_specs, check_vma=False
    )
```

time: 109 us -> 97 us (0.89)
  waiting for transfers between devices: 12.7 us -> 1.29 us
  blocking collectives: 69.5 us -> 80.5 us
  local copies, waits for them, and re-layouts: 7.43 us -> 0.83 us
  starting transfers between devices: 9.61 us -> 6.08 us
  Pallas kernels: 7.26 us -> 5.95 us
    all_to_all x3, blocking collectives: 45.2 us -> 58.2 us  [the longest x1 23.9 us: on_device(): scaled = lax.all_to_all(scaled, 'z', 0, 0, tiled=True)]
    all_to_all x1 -> x0, waiting for transfers between devices: 12.7 us -> none  [swap_sum(): v = lax.all_to_all(v, axes, 0, 0, tiled=True)]
    all_to_all x1 -> x0, starting transfers between devices: 9.61 us -> none  [swap_sum(): v = lax.all_to_all(v, axes, 0, 0, tiled=True)]
    unnamed x16 -> x2, local copies, waits for them, and re-layouts: 6.74 us -> 0.11 us
    ppermute x0 -> x1, starting transfers between devices: none -> 6.08 us  [on_device(): lax.ppermute(owned, 'yh', [(i, nyh - 1 - i) for i in range(nyh)])]
    all_gather x1 -> x0, blocking collectives: 5.99 us -> none  [on_device(): scaled = lax.all_gather(scaled, 'yh', axis=0, tiled=True)]
    all_gather x1, blocking collectives: 6.54 us -> 8.58 us  [on_device(): scaled = lax.all_gather(scaled, 'core', axis=0, tiled=True)]
    all_to_all x1, blocking collectives: 11.8 us -> 13.7 us  [on_device(): got = lax.all_to_all(local_terms, GRP, 0, 0, tiled=True)]
where the time goes in v2:
time: 97 us; the launch traced here: 95.5 us
  blocking collectives  80.5 us (83%)
  starting transfers between devices  6.08 us (6%)
  Pallas kernels  5.95 us (6%)
  waiting for transfers between devices  1.29 us (1%)
    all_to_all x1, blocking collectives, on_device(): scaled = lax.all_to_all(scaled, 'z', 0, 0, tiled=True)  23.9 us
    all_to_all x1, blocking collectives, on_device(): got = lax.all_to_all(packed.astype(jnp.float16), 'z', 0, 0, tiled=True)  22.9 us
    all_to_all x1, blocking collectives, on_device(): got = lax.all_to_all(local_terms, GRP, 0, 0, tiled=True)  13.7 us
    all_to_all x1, blocking collectives, on_device(): pair = lax.all_to_all(partial_sum, 'core', 0, 0, tiled=True)  11.5 us
    all_gather x1, blocking collectives, on_device(): scaled = lax.all_gather(scaled, 'core', axis=0, tiled=True)  8.58 us
    ppermute x1, starting transfers between devices, on_device(): lax.ppermute(owned, 'yh', [(i, nyh - 1 - i) for i in range(nyh)])  6.08 us
    pallas_call x1, Pallas kernels, on_device(): pl.pallas_call(fwd_kernel, out_shape=(jax.ShapeDtypeStruct((ncore, rows +...  3.01 us
    pallas_call x1, Pallas kernels, on_device(): pl.pallas_call(bwd_kernel, out_shape=jax.ShapeDtypeStruct((pblocks, probe...  2.89 us
  transfers between devices with their start and end apart: 1, of which 1 were waited for; matrix products, arithmetic and copies ran while one was open for 0% of the time, Pallas kernels for 0%

profile of v2, /device:TPU:1, one launch (start us, length us, event | category | flops | bytes accessed | tf_op | source)
XLA Modules:
  0.0 95.5 jit_solution(9640676950835931945)
XLA Ops:
  0.0 0.0 copy-start
  0.7 0.1 copy-done
  0.8 3.0 %fwd_blocks.1 = (f32[2,1032,128]{2,1,0:T(8,128)S(1)}, s32[1,128]{1,0:T(1,128)S(1)}, s32[1,128]{1,0:T(1,128)S(1)}) custom-call(s32[1,1]{1,0:T(1,128)S(6)} %copy.10.cnt.cnt_ref, s32[1,128]{1,0:T(1,128)} %bp_hbm.1, s32[1,128]{1,0:T(1,128)} %bo_hbm.1, bf16[32,8192]{1,0:T(8,128)(2,1)} %omega_hbm.1, bf16[1,128,128,128]{3,2,1,0:T(8,128)(2,1)} %jac_hbm.3), custom_call_target="tpu_custom_call" | custom-call | tf_op jit(solution)/shard_map/fwd_blocks/pallas_call | solution.py:118
  3.8 11.5 %all_to_all.20.pair_ref = f32[2,1032,128]{2,1,0:T(8,128)S(1)} all-to-all(f32[2,1032,128]{2,1,0:T(8,128)S(1)} %get-tuple-element.13), channel_id=1, replica_groups=mesh['x'=4,'yl'=2,'z'=16,'yh'=2,'core'=2] {'core'}, dimensions={0} | all-to-all | bytes 2113536 | tf_op jit(solution)/shard_map/all_to_all | solution.py:142
  15.3 0.1 pair_sum_scaled.1
  15.4 22.9 %all_to_all.21 = f16[16,72,128]{2,1,0:T(8,128)(2,1)S(1)} all-to-all(f16[16,72,128]{2,1,0:T(8,128)(2,1)S(1)} %convert_element_type.18), channel_id=1, replica_groups=mesh['x'=4,'yl'=2,'z'=16,'yh'=2,'core'=2] {'z'}, dimensions={0} | all-to-all | bytes 589824 | tf_op jit(solution)/shard_map/all_to_all | solution.py:151
  38.3 0.1 fusion
  38.3 6.1 %collective-permute-start = (f32[2,32,128]{2,1,0:T(8,128)S(1)}, f32[2,32,128]{2,1,0:T(8,128)S(1)}, u32[]{:S(2)}, u32[]{:S(2)}) collective-permute-start(f32[2,32,128]{2,1,0:T(8,128)S(1)} %bitcast.19), channel_id=1, source_target_pairs={{0,2},{2,0},{1,3},{3,1},{4,6},{6,4},{5,7},{7,5},{8,10},{10,8},{9,1... | collective-permute-start | bytes 98312 | tf_op jit(solution)/shard_map/ppermute | solution.py:155
  44.4 1.3 %collective-permute-done = f32[2,32,128]{2,1,0:T(8,128)S(1)} collective-permute-done((f32[2,32,128]{2,1,0:T(8,128)S(1)}, f32[2,32,128]{2,1,0:T(8,128)S(1)}, u32[]{:S(2)}, u32[]{:S(2)}) %collective-permute-start) | collective-permute-done | bytes 32800 | tf_op jit(solution)/shard_map/ppermute | solution.py:155
  45.8 23.9 %all_to_all.22 = bf16[32,32,128]{2,1,0:T(8,128)(2,1)S(1)} all-to-all(bf16[32,32,128]{2,1,0:T(8,128)(2,1)S(1)} %bitcast.18), channel_id=1, replica_groups=mesh['x'=4,'yl'=2,'z'=16,'yh'=2,'core'=2] {'z'}, dimensions={0} | all-to-all | bytes 524288 | tf_op jit(solution)/shard_map/all_to_all | solution.py:159
  69.6 8.6 %all_gather.3.v_ref = bf16[64,32,128]{2,1,0:T(8,128)(2,1)S(1)} all-gather(bf16[32,32,128]{2,1,0:T(8,128)(2,1)S(1)} %all_to_all.22), channel_id=1, replica_groups=mesh['x'=4,'yl'=2,'z'=16,'yh'=2,'core'=2] {'core'}, dimensions={0}, use_global_device_ids=true | all-gather | bytes 786432 | tf_op jit(solution)/shard_map/all_gather | solution.py:160
  78.2 2.9 %bwd_blocks.1 = bf16[64,32,128]{2,1,0:T(8,128)(2,1)S(1)} custom-call(s32[1,1]{1,0:T(1,128)S(6)} %copy.10.cnt.cnt_ref, s32[1,128]{1,0:T(1,128)S(1)} %get-tuple-element.10.bp_ref, s32[1,128]{1,0:T(1,128)S(1)} %get-tuple-element.11.bo_ref, bf16[64,32,128]{2,1,0:T(8,128)(2,1)S(1)} %all_gather.3.v_ref, bf16[1,128,128,128]{3,2,1,0:T(8,128)(2,1)} %jac_hbm.3), custom_call_target="tpu_custom_call" | custom-call | tf_op jit(solution)/shard_map/bwd_blocks/pallas_call | solution.py:162
  81.1 13.7 %all_to_all.23 = bf16[64,32,128]{2,1,0:T(8,128)(2,1)S(1)} all-to-all(bf16[64,32,128]{2,1,0:T(8,128)(2,1)S(1)} %bwd_blocks.1), channel_id=1, replica_groups=mesh['x'=4,'yl'=2,'z'=16,'yh'=2,'core'=2] {'x','yl'}, dimensions={0} | all-to-all | bytes 1048576 | tf_op jit(solution)/shard_map/all_to_all | solution.py:173
  94.8 0.1 convert_reduce_fusion
  94.9 0.7 copy_bitcast_fusion
  (5 shorter events, 0.1 us)
Async XLA Ops:
  0.0 0.8 copy-start
  38.3 7.4 %collective-permute-start = (f32[2,32,128]{2,1,0:T(8,128)S(1)}, f32[2,32,128]{2,1,0:T(8,128)S(1)}, u32[]{:S(2)}, u32[]{:S(2)}) collective-permute-start(f32[2,32,128]{2,1,0:T(8,128)S(1)} %bitcast.19), channel_id=1, source_target_pairs={{0,2},{2,0},{1,3},{3,1},{4,6},{6,4},{5,7},{7,5},{8,10},{10,8},{9,1... | collective-permute-start | bytes 98312 | tf_op jit(solution)/shard_map/ppermute | solution.py:155

commit v3 on v2

--- a/solution.py
+++ b/solution.py
@@ -25,20 +25,20 @@
     return chunk
 
 
-def fwd_kernel(cnt, bp_hbm, bo_hbm, omega_hbm, jac_hbm, out_ref, bp, bo, jac, omega, sems, jsems):
+def fwd_kernel(me, cnt, bp_hbm, bo_hbm, omega_hbm, jac_hbm, sums_ref, bp, bo, jac, omega, sems, jsems):
     width = jac.shape[1]
     probes = omega.shape[0]
-    half = (out_ref.shape[1] - SUB) // probes
+    rows = sums_ref.shape[1] - SUB
     small = [
         pltpu.make_async_copy(src, dst, sems.at[i])
         for i, (src, dst) in enumerate(((bp_hbm, bp), (bo_hbm, bo), (omega_hbm, omega)))
     ]
     for copy in small:
         copy.start()
-
     n = cnt[0, 0]
     chunk = fetch(n, jac_hbm, jac, jsems)
-    out_ref[...] = jnp.zeros_like(out_ref)
+    sums_ref[...] = jnp.zeros_like(sums_ref)
+    flip = me[0, 0] * (rows // probes // 2)
     for copy in small:
         copy.wait()
 
@@ -50,28 +50,40 @@
             panel = omega[:, pl.ds(at, width)]
             panel = jnp.where(s < n, panel, jnp.zeros_like(panel))
             term = jnp.dot(panel, jac[s], preferred_element_type=jnp.float32)
-            o = bo[0, s]
-            rows = pl.ds(pl.multiple_of((o % half) * probes, probes), probes)
-            out_ref[o // half, rows] = out_ref[o // half, rows] + term
+            o = bo[0, s] ^ flip
+            part = o // (rows // probes)
+            at = pl.ds(pl.multiple_of(o % (rows // probes) * probes, probes), probes)
+            sums_ref[part, at] = sums_ref[part, at] + term
         return carry
 
     lax.fori_loop(0, (n + CHUNK - 1) // CHUNK, step, 0)
-    body = out_ref.shape[1] - SUB
     top = jnp.zeros((SUB, width), jnp.float32)
     for i in range(2):
-        top = jnp.maximum(top, jnp.max(jnp.abs(out_ref[i, :body].reshape(body // SUB, SUB, width)), axis=0))
+        top = jnp.maximum(top, jnp.max(jnp.abs(sums_ref[i, :rows].reshape(rows // SUB, SUB, width)), axis=0))
     for i in range(2):
-        out_ref[i, body:] = top
-
-
-def pack_kernel(pair_ref, out_ref):
-    rows = pair_ref.shape[1] - SUB
+        sums_ref[i, rows:] = top
+
+
+def core_kernel(sums_ref, got_ref, mine_ref, other_ref):
+    half = mine_ref.shape[0]
+    width = mine_ref.shape[1]
+    top = sums_ref[0, 2 * half :] + got_ref[2 * half :]
+    power = jnp.clip(jnp.ceil(jnp.log2(top)), -100.0, 100.0) - 14.0
+    mine_ref[...] = sums_ref[0, :half] + got_ref[:half]
+    other = sums_ref[0, half : 2 * half] + got_ref[half : 2 * half]
+    other = other.reshape(half // SUB, SUB, width) * jnp.exp2(-power)
+    other_ref[:half] = other.reshape(half, width)
+    other_ref[half:] = power
+
+
+def chip_kernel(mine_ref, sent_ref, got_ref, out_ref):
     parts, each, width = out_ref.shape
     each = each - SUB
-    top = pair_ref[0, rows:] + pair_ref[1, rows:]
-    power = jnp.clip(jnp.ceil(jnp.log2(top)), -100.0, 100.0) - 14.0
-    data = pair_ref[0, :rows] + pair_ref[1, :rows]
-    data = data.reshape(rows // SUB, SUB, width) * jnp.exp2(-power)
+    half = mine_ref.shape[0]
+    theirs = got_ref[half:]
+    power = jnp.maximum(sent_ref[half:], theirs) + 1.0
+    got = got_ref[:half].reshape(half // SUB, SUB, width) * jnp.exp2(theirs - power)
+    data = mine_ref[...].reshape(half // SUB, SUB, width) * jnp.exp2(-power) + got
     out_ref[:, :each] = data.reshape(parts, each, width)
     out_ref[:, each:] = jnp.broadcast_to(power, (parts, SUB, width))
 
@@ -107,6 +119,7 @@
     smem = pl.BlockSpec(memory_space=pltpu.SMEM)
     vmem = pl.BlockSpec(memory_space=pltpu.VMEM)
     hbm = pl.BlockSpec(memory_space=pltpu.HBM)
+    little = pltpu.CompilerParams(vmem_limit_bytes=8 << 20)
     params = pltpu.CompilerParams(vmem_limit_bytes=24 << 20)
     blocks = pltpu.VMEM((slots, width, width), jac_blocks.dtype)
     done = pltpu.SemaphoreType.DMA((slots // CHUNK,))
@@ -115,14 +128,22 @@
         for a in (block_param, block_obs, omega, jac_blocks)
     ]
     rows = oblocks // ncore * probes
-    partial_sum, bp, bo = pl.pallas_call(
+    each = oblocks // (nz * nyh * ncore) * probes
+    per = each // probes
+    quarter = lax.axis_index("core") * nyh + lax.axis_index("yh")
+    weight = lax.dynamic_slice(
+        obs_weight.reshape(oblocks, 1, width),
+        ((quarter * nz + lax.axis_index("z")) * per, 0, 0),
+        (per, 1, width),
+    )
+    sums, bp, bo = pl.pallas_call(
         fwd_kernel,
         out_shape=(
             jax.ShapeDtypeStruct((ncore, rows + SUB, width), jnp.float32),
             jax.ShapeDtypeStruct(block_param.shape, jnp.int32),
             jax.ShapeDtypeStruct(block_obs.shape, jnp.int32),
         ),
-        in_specs=[smem] + [hbm] * 4,
+        in_specs=[smem] * 2 + [hbm] * 4,
         out_specs=(vmem, smem, smem),
         scratch_shapes=[
             blocks,
@@ -132,31 +153,39 @@
         ],
         compiler_params=params,
         name="fwd_blocks",
-    )(block_count, *held)
-
-    each = rows // nz
-    per = each // probes
-    first = (lax.axis_index("core") * nz + lax.axis_index("z")) * per
-    weight = lax.dynamic_slice(obs_weight.reshape(oblocks, 1, width), (first, 0, 0), (per, 1, width))
-    partial_sum, weight = lax.optimization_barrier((partial_sum, weight))
-    pair = lax.all_to_all(partial_sum, "core", 0, 0, tiled=True)
+    )(quarter.reshape(1, 1), block_count, *held)
+    sums, weight = lax.optimization_barrier((sums, weight))
+
+    swap = [(i, 1 - i) for i in range(2)]
+    mine, other = pl.pallas_call(
+        core_kernel,
+        out_shape=(
+            jax.ShapeDtypeStruct((rows // nyh, width), jnp.float32),
+            jax.ShapeDtypeStruct((rows // nyh + SUB, width), jnp.float32),
+        ),
+        in_specs=[vmem] * 2,
+        out_specs=(vmem, vmem),
+        compiler_params=little,
+        name="add_core",
+    )(sums, lax.ppermute(sums[1], "core", swap))
+    got = lax.ppermute(other.astype(jnp.float16), "yh", swap).astype(jnp.float32)
     packed = pl.pallas_call(
-        pack_kernel,
+        chip_kernel,
         out_shape=jax.ShapeDtypeStruct((nz, each + SUB, width), jnp.float32),
-        in_specs=[vmem],
+        in_specs=[vmem] * 3,
         out_specs=vmem,
-        compiler_params=pltpu.CompilerParams(vmem_limit_bytes=8 << 20),
-        name="pair_sum_scaled",
-    )(pair)
+        compiler_params=little,
+        name="add_chip",
+    )(mine, other, got)
     got = lax.all_to_all(packed.astype(jnp.float16), "z", 0, 0, tiled=True)
     scale = jnp.exp2(got[:, each:].astype(jnp.float32))
     data = got[:, :each].astype(jnp.float32).reshape(nz, each // SUB, SUB, width)
-    owned = jnp.sum(data * scale[:, None], axis=0).reshape(each // probes, probes, width)
-    owned = owned + lax.ppermute(owned, "yh", [(i, nyh - 1 - i) for i in range(nyh)])
+    owned = jnp.sum(data * scale[:, None], axis=0).reshape(per, probes, width)
 
     scaled = (owned * weight).astype(jnp.bfloat16)
     scaled = jnp.broadcast_to(scaled, (nz, per, probes, width)).reshape(nz * per, probes, width)
     scaled = lax.all_to_all(scaled, "z", 0, 0, tiled=True)
+    scaled = lax.all_gather(scaled, "yh", axis=0, tiled=True)
     scaled = lax.all_gather(scaled, "core", axis=0, tiled=True)
 
     local_terms = pl.pallas_call(

time: 97 us -> 95.2 us (0.981)
  blocking collectives: 80.5 us -> 68.2 us
  waiting for transfers between devices: 1.29 us -> 7.74 us
  starting transfers between devices: 6.08 us -> 11.5 us
    all_to_all x1 -> x0, blocking collectives: 11.5 us -> none  [on_device(): pair = lax.all_to_all(partial_sum, 'core', 0, 0, tiled=True)]
    ppermute x1 -> x2, waiting for transfers between devices: 1.29 us -> 7.74 us  [the longest x1 6.22 us: on_device(): lax.ppermute(other.astype(jnp.float16), 'yh', swap).astype(jnp.float32)]
    all_gather x0 -> x1, blocking collectives: none -> 5.99 us  [on_device(): scaled = lax.all_gather(scaled, 'yh', axis=0, tiled=True)]
    ppermute x1 -> x2, starting transfers between devices: 6.08 us -> 11.5 us  [the longest x1 9.63 us: on_device(): lax.ppermute(sums[1], 'core', swap)]
    all_to_all x1, blocking collectives: 23.9 us -> 18.5 us  [on_device(): scaled = lax.all_to_all(scaled, 'z', 0, 0, tiled=True)]
    all_gather x1, blocking collectives: 8.58 us -> 6.94 us  [on_device(): scaled = lax.all_gather(scaled, 'core', axis=0, tiled=True)]
  transfers between devices with their start and end apart: 1 -> 2, of which waited for: 1 -> 2; matrix products, arithmetic and copies ran while one was open for 0% -> 0% of each run, Pallas kernels for 0% -> 0%
where the time goes in v3:
time: 95.2 us; the launch traced here: 94.5 us
  blocking collectives  68.2 us (72%)
  starting transfers between devices  11.5 us (12%)
  waiting for transfers between devices  7.74 us (8%)
  Pallas kernels  5.2 us (5%)
    all_to_all x1, blocking collectives, on_device(): got = lax.all_to_all(packed.astype(jnp.float16), 'z', 0, 0, tiled=True)  22.6 us
    all_to_all x1, blocking collectives, on_device(): scaled = lax.all_to_all(scaled, 'z', 0, 0, tiled=True)  18.5 us
    all_to_all x1, blocking collectives, on_device(): got = lax.all_to_all(local_terms, GRP, 0, 0, tiled=True)  14.2 us
    ppermute x1, starting transfers between devices, on_device(): lax.ppermute(sums[1], 'core', swap)  9.63 us
    all_gather x1, blocking collectives, on_device(): scaled = lax.all_gather(scaled, 'core', axis=0, tiled=True)  6.94 us
    ppermute x1, waiting for transfers between devices, on_device(): lax.ppermute(other.astype(jnp.float16), 'yh', swap).astype(jnp.float32)  6.22 us
    all_gather x1, blocking collectives, on_device(): scaled = lax.all_gather(scaled, 'yh', axis=0, tiled=True)  5.99 us
    pallas_call x1, Pallas kernels, on_device(): pl.pallas_call(fwd_kernel, out_shape=(jax.ShapeDtypeStruct((ncore, rows +...  2.58 us
  transfers between devices with their start and end apart: 2, of which 2 were waited for; matrix products, arithmetic and copies ran while one was open for 0% of the time, Pallas kernels for 0%

profile of v3, /device:TPU:1, one launch (start us, length us, event | category | flops | bytes accessed | tf_op | source)
XLA Modules:
  0.0 94.5 jit_solution(6786923843031401454)
XLA Ops:
  0.0 0.0 copy-start
  0.7 0.1 copy-done
  0.8 2.6 %fwd_blocks.1 = (f32[2,1032,128]{2,1,0:T(8,128)S(1)}, s32[1,128]{1,0:T(1,128)S(1)}, s32[1,128]{1,0:T(1,128)S(1)}) custom-call(s32[1,1]{1,0:T(1,128)} %bitcast.me, s32[1,1]{1,0:T(1,128)S(6)} %copy.13.cnt.cnt_ref, s32[1,128]{1,0:T(1,128)} %bp_hbm.1, s32[1,128]{1,0:T(1,128)} %bo_hbm.1, bf16[32,8192]{1,0:T(8,128)(2,1)} %omega_hbm.1, ...), custom_call_target="tpu_custom_call" | custom-call | tf_op jit(solution)/shard_map/fwd_blocks/pallas_call | solution.py:139
  3.4 9.6 %collective-permute-start = (f32[1032,128]{1,0:T(8,128)S(1)}, f32[1032,128]{1,0:T(8,128)S(1)}, u32[]{:S(2)}, u32[]{:S(2)}) collective-permute-start(f32[1032,128]{1,0:T(8,128)S(1)} %slice_bitcast_fusion), channel_id=1, source_target_pairs={{0,1},{1,0},{2,3},{3,2},{4,5},{5,4},{6,7},{7,6},{8,9},{9,8},{10,11... | collective-permute-start | bytes 1585160 | tf_op jit(solution)/shard_map/ppermute | solution.py:170
  13.0 1.5 %collective-permute-done.got_ref = f32[1032,128]{1,0:T(8,128)S(1)} collective-permute-done((f32[1032,128]{1,0:T(8,128)S(1)}, f32[1032,128]{1,0:T(8,128)S(1)}, u32[]{:S(2)}, u32[]{:S(2)}) %collective-permute-start) | collective-permute-done | bytes 528416 | tf_op jit(solution)/shard_map/ppermute | solution.py:170
  14.6 0.1 add_core.1
  14.7 1.9 %collective-permute-start.1 = (f16[520,128]{1,0:T(8,128)(2,1)S(1)}, f16[520,128]{1,0:T(8,128)(2,1)S(1)}, u32[]{:S(2)}, u32[]{:S(2)}) collective-permute-start(f16[520,128]{1,0:T(8,128)(2,1)S(1)} %convert_element_type.27), channel_id=1, source_target_pairs={{0,2},{2,0},{1,3},{3,1},{4,6},{6,4},{5,7},{7,5},{8,10},{10,8},{9,1... | collective-permute-start | bytes 399368 | tf_op jit(solution)/shard_map/ppermute | solution.py:171
  16.6 6.2 %collective-permute-done.1 = f16[520,128]{1,0:T(8,128)(2,1)S(1)} collective-permute-done((f16[520,128]{1,0:T(8,128)(2,1)S(1)}, f16[520,128]{1,0:T(8,128)(2,1)S(1)}, u32[]{:S(2)}, u32[]{:S(2)}) %collective-permute-start.1) | collective-permute-done | bytes 133152 | tf_op jit(solution)/shard_map/ppermute | solution.py:171
  22.8 0.1 add_chip.1
  22.9 22.6 %all_to_all.15 = f16[16,40,128]{2,1,0:T(8,128)(2,1)S(1)} all-to-all(f16[16,40,128]{2,1,0:T(8,128)(2,1)S(1)} %convert_element_type.29), channel_id=1, replica_groups=mesh['x'=4,'yl'=2,'z'=16,'yh'=2,'core'=2] {'z'}, dimensions={0} | all-to-all | bytes 327680 | tf_op jit(solution)/shard_map/all_to_all | solution.py:180
  45.6 18.5 %all_to_all.16 = bf16[16,32,128]{2,1,0:T(8,128)(2,1)S(1)} all-to-all(bf16[16,32,128]{2,1,0:T(8,128)(2,1)S(1)} %reshape.42), channel_id=1, replica_groups=mesh['x'=4,'yl'=2,'z'=16,'yh'=2,'core'=2] {'z'}, dimensions={0} | all-to-all | bytes 262144 | tf_op jit(solution)/shard_map/all_to_all | solution.py:187
  64.1 6.0 %all_gather.6 = bf16[32,32,128]{2,1,0:T(8,128)(2,1)S(1)} all-gather(bf16[16,32,128]{2,1,0:T(8,128)(2,1)S(1)} %all_to_all.16), channel_id=1, replica_groups=mesh['x'=4,'yl'=2,'z'=16,'yh'=2,'core'=2] {'yh'}, dimensions={0}, use_global_device_ids=true | all-gather | bytes 393216 | tf_op jit(solution)/shard_map/all_gather | solution.py:188
  70.1 6.9 %all_gather.7.v_ref = bf16[64,32,128]{2,1,0:T(8,128)(2,1)S(1)} all-gather(bf16[32,32,128]{2,1,0:T(8,128)(2,1)S(1)} %all_gather.6), channel_id=1, replica_groups=mesh['x'=4,'yl'=2,'z'=16,'yh'=2,'core'=2] {'core'}, dimensions={0}, use_global_device_ids=true | all-gather | bytes 786432 | tf_op jit(solution)/shard_map/all_gather | solution.py:189
  77.1 2.5 %bwd_blocks.1 = bf16[64,32,128]{2,1,0:T(8,128)(2,1)S(1)} custom-call(s32[1,1]{1,0:T(1,128)S(6)} %copy.13.cnt.cnt_ref, s32[1,128]{1,0:T(1,128)S(1)} %get-tuple-element.12.bp_ref, s32[1,128]{1,0:T(1,128)S(1)} %get-tuple-element.13.bo_ref, bf16[64,32,128]{2,1,0:T(8,128)(2,1)S(1)} %all_gather.7.v_ref, bf16[1,128,128,128]{3,2,1,0:T(8,128)(2,1)} %jac_hbm.3), custom_call_target="tpu_custom_call" | custom-call | tf_op jit(solution)/shard_map/bwd_blocks/pallas_call | solution.py:191
  79.6 14.2 %all_to_all.17 = bf16[64,32,128]{2,1,0:T(8,128)(2,1)S(1)} all-to-all(bf16[64,32,128]{2,1,0:T(8,128)(2,1)S(1)} %bwd_blocks.1), channel_id=1, replica_groups=mesh['x'=4,'yl'=2,'z'=16,'yh'=2,'core'=2] {'x','yl'}, dimensions={0} | all-to-all | bytes 1048576 | tf_op jit(solution)/shard_map/all_to_all | solution.py:202
  93.7 0.1 convert_reduce_fusion
  93.8 0.7 copy_bitcast_fusion
  (9 shorter events, 0.2 us)
Async XLA Ops:
  0.0 0.8 copy-start
  3.4 11.2 %collective-permute-start = (f32[1032,128]{1,0:T(8,128)S(1)}, f32[1032,128]{1,0:T(8,128)S(1)}, u32[]{:S(2)}, u32[]{:S(2)}) collective-permute-start(f32[1032,128]{1,0:T(8,128)S(1)} %slice_bitcast_fusion), channel_id=1, source_target_pairs={{0,1},{1,0},{2,3},{3,2},{4,5},{5,4},{6,7},{7,6},{8,9},{9,8},{10,11... | collective-permute-start | bytes 1585160 | tf_op jit(solution)/shard_map/ppermute | solution.py:170
  14.7 8.2 %collective-permute-start.1 = (f16[520,128]{1,0:T(8,128)(2,1)S(1)}, f16[520,128]{1,0:T(8,128)(2,1)S(1)}, u32[]{:S(2)}, u32[]{:S(2)}) collective-permute-start(f16[520,128]{1,0:T(8,128)(2,1)S(1)} %convert_element_type.27), channel_id=1, source_target_pairs={{0,2},{2,0},{1,3},{3,1},{4,6},{6,4},{5,7},{7,5},{8,10},{10,8},{9,1... | collective-permute-start | bytes 399368 | tf_op jit(solution)/shard_map/ppermute | solution.py:171

commit v4 on v3

v4 whole, which is shorter than its diff:
```python
import jax
import jax.numpy as jnp
from jax import lax
from jax.experimental import pallas as pl
from jax.experimental.pallas import tpu as pltpu
from jax.sharding import Mesh, PartitionSpec as P

CHUNK = 64
FETCH = 16
SUB = 8
PAR = ("z", "yh", "core")
GRP = ("x", "yl")


def fwd_kernel(
    me, cnt, bp_hbm, bo_hbm, omega_hbm, jac_hbm, sums_ref, jac, bp, bo, omega, sems, jsems
):
    width = jac.shape[1]
    probes = omega.shape[0]
    rows = sums_ref.shape[1] - SUB
    half = rows // probes
    small = [
        pltpu.make_async_copy(src, dst, sems.at[i])
        for i, (src, dst) in enumerate(((bp_hbm, bp), (bo_hbm, bo), (omega_hbm, omega)))
    ]
    for copy in small:
        copy.start()
    n = cnt[0, 0]

    def piece(c):
        at = pl.ds(c * FETCH, FETCH)
        return pltpu.make_async_copy(jac_hbm.at[0, at], jac.at[at], jsems.at[c])

    def each_piece(act):
        for first in range(0, jac.shape[0], CHUNK):
            pieces = range(first // FETCH, (first + CHUNK) // FETCH)
            if first:

                @pl.when(first < n)
                def _():
                    for c in pieces:
                        act(c, first + CHUNK)
            else:
                for c in pieces:
                    act(c, first + CHUNK)

    each_piece(lambda c, end: piece(c).start())
    sums_ref[...] = jnp.zeros_like(sums_ref)
    for copy in small:
        copy.wait()

    def use(c, end):
        piece(c).wait()
        for s in range(c * FETCH, (c + 1) * FETCH):
            at = pl.multiple_of(bp[0, s] * width, width)
            panel = omega[:, pl.ds(at, width)]
            panel = jnp.where(s < n, panel, jnp.zeros_like(panel))
            term = jnp.dot(panel, jac[s], preferred_element_type=jnp.float32)
            o = bo[0, s]
            part = (o // half) ^ me[0, 0]
            row = (o % (half // 2)) * 2 + o // (half // 2) % 2
            at = pl.ds(pl.multiple_of(row * probes, probes), probes)
            sums_ref[part, at] = sums_ref[part, at] + term

    each_piece(use)
    top = jnp.zeros((SUB, width), jnp.float32)
    for i in range(2):
        top = jnp.maximum(top, jnp.max(jnp.abs(sums_ref[i, :rows].reshape(rows // SUB, SUB, width)), axis=0))
    for i in range(2):
        sums_ref[i, rows:] = top


def core_kernel(sums_ref, got_ref, out_ref):
    parts, each, width = out_ref.shape
    each = each - SUB
    rows = parts * each
    top = sums_ref[0, rows:] + got_ref[rows:]
    power = jnp.clip(jnp.ceil(jnp.log2(top)), -100.0, 100.0) - 14.0
    data = (sums_ref[0, :rows] + got_ref[:rows]).reshape(rows // SUB, SUB, width) * jnp.exp2(-power)
    out_ref[:, :each] = data.reshape(parts, each, width)
    out_ref[:, each:] = jnp.broadcast_to(power, (parts, SUB, width))


def bwd_kernel(cnt, bp, bo, v_ref, jac, out_ref, acc):
    width = jac.shape[1]
    probes = v_ref.shape[1]
    n = cnt[0, 0]
    acc[...] = jnp.zeros_like(acc)

    def step(c, carry):
        for j in range(0, CHUNK, 2):
            first = c * CHUNK + j
            pair = []
            for s in (first, first + 1):
                v = v_ref[bo[0, s]]
                pair.append(jnp.where(s < n, v, jnp.zeros_like(v)))
            blocks = jac[pl.ds(first, 2)].reshape(2 * width, width)
            terms = lax.dot_general(
                jnp.concatenate(pair, axis=0),
                blocks,
                (((1,), (1,)), ((), ())),
                preferred_element_type=jnp.float32,
            )
            for i in range(2):
                p = bp[0, first + i]
                acc[p] = acc[p] + terms[i * probes : (i + 1) * probes, i * width : (i + 1) * width]
        return carry

    lax.fori_loop(0, (n + CHUNK - 1) // CHUNK, step, 0)
    out_ref[...] = acc[...].astype(out_ref.dtype)


def on_device(omega, jac_blocks, block_param, block_obs, block_count, obs_weight):
    probes = omega.shape[0]
    slots, width = jac_blocks.shape[1], jac_blocks.shape[2]
    pblocks = omega.shape[1] // width
    oblocks = obs_weight.shape[1] // width
    nz, nyh, ncore = (lax.axis_size(a) for a in PAR)
    smem = pl.BlockSpec(memory_space=pltpu.SMEM)
    vmem = pl.BlockSpec(memory_space=pltpu.VMEM)
    hbm = pl.BlockSpec(memory_space=pltpu.HBM)
    little = pltpu.CompilerParams(vmem_limit_bytes=8 << 20)
    params = pltpu.CompilerParams(vmem_limit_bytes=24 << 20)
    held = [
        pltpu.with_memory_space_constraint(a, pltpu.HBM)
        for a in (block_param, block_obs, omega, jac_blocks)
    ]
    rows = oblocks // ncore * probes
    each = oblocks // (nz * nyh * ncore) * probes
    per = each // probes
    quarter = lax.axis_index("core") * nyh + lax.axis_index("yh")
    weight = lax.dynamic_slice(
        obs_weight.reshape(oblocks, 1, width),
        ((quarter * nz + lax.axis_index("z")) * per, 0, 0),
        (per, 1, width),
    )
    sums, jac, bp, bo = pl.pallas_call(
        fwd_kernel,
        out_shape=(
            jax.ShapeDtypeStruct((ncore, rows + SUB, width), jnp.float32),
            jax.ShapeDtypeStruct((slots, width, width), jac_blocks.dtype),
            jax.ShapeDtypeStruct(block_param.shape, jnp.int32),
            jax.ShapeDtypeStruct(block_obs.shape, jnp.int32),
        ),
        in_specs=[smem] * 2 + [hbm] * 4,
        out_specs=(vmem, vmem, smem, smem),
        scratch_shapes=[
            pltpu.VMEM(omega.shape, omega.dtype),
            pltpu.SemaphoreType.DMA((3,)),
            pltpu.SemaphoreType.DMA((slots // FETCH,)),
        ],
        compiler_params=params,
        name="fwd_blocks",
    )(lax.axis_index("core").reshape(1, 1), block_count, *held)
    sums, weight = lax.optimization_barrier((sums, weight))

    packed = pl.pallas_call(
        core_kernel,
        out_shape=jax.ShapeDtypeStruct((nz * nyh, each + SUB, width), jnp.float32),
        in_specs=[vmem] * 2,
        out_specs=vmem,
        compiler_params=little,
        name="add_core",
    )(sums, lax.ppermute(sums[1], "core", [(0, 1), (1, 0)]))
    got = lax.all_to_all(packed.astype(jnp.float16), ("z", "yh"), 0, 0, tiled=True)
    scale = jnp.exp2(got[:, each:].astype(jnp.float32))
    data = got[:, :each].astype(jnp.float32).reshape(nz * nyh, each // SUB, SUB, width)
    owned = jnp.sum(data * scale[:, None], axis=0).reshape(per, probes, width)

    scaled = (owned * weight).astype(jnp.bfloat16)
    scaled = jnp.broadcast_to(scaled, (nz, per, probes, width)).reshape(nz * per, probes, width)
    scaled = lax.all_to_all(scaled, "z", 0, 0, tiled=True)
    scaled = lax.all_gather(scaled, "yh", axis=0, tiled=True)
    scaled = lax.all_gather(scaled, "core", axis=0, tiled=True)

    local_terms = pl.pallas_call(
        bwd_kernel,
        out_shape=jax.ShapeDtypeStruct((pblocks, probes, width), jnp.bfloat16),
        in_specs=[smem, smem, smem, vmem, vmem],
        out_specs=vmem,
        scratch_shapes=[pltpu.VMEM((pblocks, probes, width), jnp.float32)],
        compiler_params=params,
        name="bwd_blocks",
    )(block_count, bp, bo, scaled, jac)

    n = lax.axis_size(GRP)
    got = lax.all_to_all(local_terms, GRP, 0, 0, tiled=True)
    got = got.reshape(n, pblocks // n, probes, width).astype(jnp.float32)
    total = jnp.sum(got, axis=0)
    return jnp.transpose(total, (1, 0, 2)).reshape(probes, pblocks // n * width)


def solution(mesh):
    mesh = Mesh(mesh.devices.reshape(4, 2, 16, 2, 2), GRP + PAR)
    in_specs = (
        P(None, PAR),
        P(GRP, PAR, None, None),
        P(GRP, PAR),
        P(GRP, PAR),
        P(GRP, PAR),
        P(GRP, None),
    )
    out_specs = P(None, PAR + GRP)
    return jax.shard_map(
        on_device, mesh=mesh, in_specs=in_specs, out_specs=out_specs, check_vma=False
    )
```

time: 95.2 us -> 95.6 us (level)
  blocking collectives: 68.2 us -> 77.9 us
  waiting for transfers between devices: 7.74 us -> 1.52 us
  starting transfers between devices: 11.5 us -> 8.78 us
    all_to_all x1, blocking collectives: 22.6 us -> 36 us  [on_device(): lax.all_to_all(packed.astype(jnp.float16), ('z', 'yh'), 0, 0, tiled=True)]
    ppermute x2 -> x1, waiting for transfers between devices: 7.74 us -> 1.52 us  [on_device(): lax.ppermute(sums[1], 'core', [(0, 1), (1, 0)])]
    ppermute x2 -> x1, starting transfers between devices: 11.5 us -> 8.78 us  [on_device(): lax.ppermute(sums[1], 'core', [(0, 1), (1, 0)])]
    all_to_all x1, blocking collectives: 18.5 us -> 16.3 us  [on_device(): scaled = lax.all_to_all(scaled, 'z', 0, 0, tiled=True)]
    all_to_all x1, blocking collectives: 14.2 us -> 12.8 us  [on_device(): got = lax.all_to_all(local_terms, GRP, 0, 0, tiled=True)]
    pallas_call x1, Pallas kernels: 2.49 us -> 1.52 us  [on_device(): pl.pallas_call(bwd_kernel, out_shape=jax.ShapeDtypeStruct((pblocks, probe...]
  transfers between devices with their start and end apart: 2 -> 1, of which waited for: 2 -> 1; matrix products, arithmetic and copies ran while one was open for 0% -> 0% of each run, Pallas kernels for 0% -> 0%
where the time goes in v4:
time: 95.6 us; the launch traced here: 95 us
  blocking collectives  77.9 us (81%)
  starting transfers between devices  8.78 us (9%)
  Pallas kernels  5.07 us (5%)
  waiting for transfers between devices  1.52 us (2%)
    all_to_all x1, blocking collectives, on_device(): lax.all_to_all(packed.astype(jnp.float16), ('z', 'yh'), 0, 0, tiled=True)  36 us
    all_to_all x1, blocking collectives, on_device(): scaled = lax.all_to_all(scaled, 'z', 0, 0, tiled=True)  16.3 us
    all_to_all x1, blocking collectives, on_device(): got = lax.all_to_all(local_terms, GRP, 0, 0, tiled=True)  12.8 us
    ppermute x1, starting transfers between devices, on_device(): lax.ppermute(sums[1], 'core', [(0, 1), (1, 0)])  8.78 us
    all_gather x1, blocking collectives, on_device(): scaled = lax.all_gather(scaled, 'core', axis=0, tiled=True)  6.79 us
    all_gather x1, blocking collectives, on_device(): scaled = lax.all_gather(scaled, 'yh', axis=0, tiled=True)  5.99 us
    pallas_call x1, Pallas kernels, on_device(): pl.pallas_call(fwd_kernel, out_shape=(jax.ShapeDtypeStruct((ncore, rows +...  3.48 us
  transfers between devices with their start and end apart: 1, of which 1 were waited for; matrix products, arithmetic and copies ran while one was open for 0% of the time, Pallas kernels for 0%

profile of v4, /device:TPU:1, one launch (start us, length us, event | category | flops | bytes accessed | tf_op | source)
XLA Modules:
  0.0 95.0 jit_solution(17639115138829582567)
XLA Ops:
  0.0 0.0 copy-start
  0.7 0.1 copy-done
  0.8 3.5 %fwd_blocks.1 = (f32[2,1032,128]{2,1,0:T(8,128)S(1)}, bf16[128,128,128]{2,1,0:T(8,128)(2,1)S(1)}, s32[1,128]{1,0:T(1,128)S(1)}, s32[1,128]{1,0:T(1,128)S(1)}) custom-call(s32[1,1]{1,0:T(1,128)} %bitcast.me, s32[1,1]{1,0:T(1,128)S(6)} %copy.13.cnt, s32[1,128]{1,0:T(1,128)} %bp_hbm.1, s32[1,128]{1,0:T(1,128)} %bo_hbm.1, bf16[32,8192]{1,0:T(8,128)(2,1)} %omega_hbm.1, ...), custom_call_target="tpu_custom_call" | custom-call | tf_op jit(solution)/shard_map/fwd_blocks/pallas_call | solution.py:137
  4.3 8.8 %collective-permute-start = (f32[1032,128]{1,0:T(8,128)S(1)}, f32[1032,128]{1,0:T(8,128)S(1)}, u32[]{:S(2)}, u32[]{:S(2)}) collective-permute-start(f32[1032,128]{1,0:T(8,128)S(1)} %slice_bitcast_fusion), channel_id=1, source_target_pairs={{0,1},{1,0},{2,3},{3,2},{4,5},{5,4},{6,7},{7,6},{8,9},{9,8},{10,11... | collective-permute-start | bytes 1585160 | tf_op jit(solution)/shard_map/ppermute | solution.py:164
  13.1 1.5 %collective-permute-done.got_ref = f32[1032,128]{1,0:T(8,128)S(1)} collective-permute-done((f32[1032,128]{1,0:T(8,128)S(1)}, f32[1032,128]{1,0:T(8,128)S(1)}, u32[]{:S(2)}, u32[]{:S(2)}) %collective-permute-start) | collective-permute-done | bytes 528416 | tf_op jit(solution)/shard_map/ppermute | solution.py:164
  14.6 0.1 add_core.1
  14.7 36.0 %all_to_all.15 = f16[32,40,128]{2,1,0:T(8,128)(2,1)S(1)} all-to-all(f16[32,40,128]{2,1,0:T(8,128)(2,1)S(1)} %convert_element_type.21), channel_id=1, replica_groups=mesh['x'=4,'yl'=2,'z'=16,'yh'=2,'core'=2] {'z','yh'}, dimensions={0} | all-to-all | bytes 655360 | tf_op jit(solution)/shard_map/all_to_all | solution.py:165
  50.7 0.1 fusion
  50.9 16.3 %all_to_all.16 = bf16[16,32,128]{2,1,0:T(8,128)(2,1)S(1)} all-to-all(bf16[16,32,128]{2,1,0:T(8,128)(2,1)S(1)} %reshape.42), channel_id=1, replica_groups=mesh['x'=4,'yl'=2,'z'=16,'yh'=2,'core'=2] {'z'}, dimensions={0} | all-to-all | bytes 262144 | tf_op jit(solution)/shard_map/all_to_all | solution.py:172
  67.1 6.0 %all_gather.6 = bf16[32,32,128]{2,1,0:T(8,128)(2,1)S(1)} all-gather(bf16[16,32,128]{2,1,0:T(8,128)(2,1)S(1)} %all_to_all.16), channel_id=1, replica_groups=mesh['x'=4,'yl'=2,'z'=16,'yh'=2,'core'=2] {'yh'}, dimensions={0}, use_global_device_ids=true | all-gather | bytes 393216 | tf_op jit(solution)/shard_map/all_gather | solution.py:173
  73.1 6.8 %all_gather.7.v_ref = bf16[64,32,128]{2,1,0:T(8,128)(2,1)S(1)} all-gather(bf16[32,32,128]{2,1,0:T(8,128)(2,1)S(1)} %all_gather.6), channel_id=1, replica_groups=mesh['x'=4,'yl'=2,'z'=16,'yh'=2,'core'=2] {'core'}, dimensions={0}, use_global_device_ids=true | all-gather | bytes 786432 | tf_op jit(solution)/shard_map/all_gather | solution.py:174
  79.9 1.5 %bwd_blocks.1 = bf16[64,32,128]{2,1,0:T(8,128)(2,1)S(1)} custom-call(s32[1,1]{1,0:T(1,128)S(6)} %copy.13.cnt, s32[1,128]{1,0:T(1,128)S(1)} %get-tuple-element.11.bp, s32[1,128]{1,0:T(1,128)S(1)} %get-tuple-element.12.bo, bf16[64,32,128]{2,1,0:T(8,128)(2,1)S(1)} %all_gather.7.v_ref, bf16[128,128,128]{2,1,0:T(8,128)(2,1)S(1)} %get-tuple-element.16.jac), custom_call_target="tpu_custom_call" | custom-call | tf_op jit(solution)/shard_map/bwd_blocks/pallas_call | solution.py:176
  81.4 12.8 %all_to_all.17 = bf16[64,32,128]{2,1,0:T(8,128)(2,1)S(1)} all-to-all(bf16[64,32,128]{2,1,0:T(8,128)(2,1)S(1)} %bwd_blocks.1), channel_id=1, replica_groups=mesh['x'=4,'yl'=2,'z'=16,'yh'=2,'core'=2] {'x','yl'}, dimensions={0} | all-to-all | bytes 1048576 | tf_op jit(solution)/shard_map/all_to_all | solution.py:187
  94.3 0.1 convert_reduce_fusion
  94.3 0.7 copy_bitcast_fusion
  (6 shorter events, 0.1 us)
Async XLA Ops:
  0.0 0.8 copy-start
  4.3 10.3 %collective-permute-start = (f32[1032,128]{1,0:T(8,128)S(1)}, f32[1032,128]{1,0:T(8,128)S(1)}, u32[]{:S(2)}, u32[]{:S(2)}) collective-permute-start(f32[1032,128]{1,0:T(8,128)S(1)} %slice_bitcast_fusion), channel_id=1, source_target_pairs={{0,1},{1,0},{2,3},{3,2},{4,5},{5,4},{6,7},{7,6},{8,9},{9,8},{10,11... | collective-permute-start | bytes 1585160 | tf_op jit(solution)/shard_map/ppermute | solution.py:164

commit v5 on v3

--- a/solution.py
+++ b/solution.py
@@ -5,30 +5,19 @@
 from jax.experimental.pallas import tpu as pltpu
 from jax.sharding import Mesh, PartitionSpec as P
 
-CHUNK = 16
+CHUNK = 64
 SUB = 8
 PAR = ("z", "yh", "core")
 GRP = ("x", "yl")
 
 
-def fetch(n, jac_hbm, jac, sems):
-    def chunk(c):
-        at = pl.ds(pl.multiple_of(c * CHUNK, CHUNK), CHUNK)
-        return pltpu.make_async_copy(jac_hbm.at[0, at], jac.at[at], sems.at[c])
-
-    for c in range(jac.shape[0] // CHUNK):
-
-        @pl.when(c * CHUNK < n)
-        def _():
-            chunk(c).start()
-
-    return chunk
-
-
-def fwd_kernel(me, cnt, bp_hbm, bo_hbm, omega_hbm, jac_hbm, sums_ref, bp, bo, jac, omega, sems, jsems):
+def fwd_kernel(
+    me, cnt, bp_hbm, bo_hbm, omega_hbm, jac_hbm, sums_ref, jac, bp, bo, omega, sems, jsems
+):
     width = jac.shape[1]
     probes = omega.shape[0]
     rows = sums_ref.shape[1] - SUB
+    half = rows // probes
     small = [
         pltpu.make_async_copy(src, dst, sems.at[i])
         for i, (src, dst) in enumerate(((bp_hbm, bp), (bo_hbm, bo), (omega_hbm, omega)))
@@ -36,9 +25,19 @@
     for copy in small:
         copy.start()
     n = cnt[0, 0]
-    chunk = fetch(n, jac_hbm, jac, jsems)
+
+    def chunk(c):
+        at = pl.ds(pl.multiple_of(c * CHUNK, CHUNK), CHUNK)
+        return pltpu.make_async_copy(jac_hbm.at[0, at], jac.at[at], jsems.at[c])
+
+    for c in range(jac.shape[0] // CHUNK):
+
+        @pl.when(c * CHUNK < n)
+        def _():
+            chunk(c).start()
+
     sums_ref[...] = jnp.zeros_like(sums_ref)
-    flip = me[0, 0] * (rows // probes // 2)
+    flip = me[0, 0] * (half // 2)
     for copy in small:
         copy.wait()
 
@@ -51,9 +50,8 @@
             panel = jnp.where(s < n, panel, jnp.zeros_like(panel))
             term = jnp.dot(panel, jac[s], preferred_element_type=jnp.float32)
             o = bo[0, s] ^ flip
-            part = o // (rows // probes)
-            at = pl.ds(pl.multiple_of(o % (rows // probes) * probes, probes), probes)
-            sums_ref[part, at] = sums_ref[part, at] + term
+            at = pl.ds(pl.multiple_of(o % half * probes, probes), probes)
+            sums_ref[o // half, at] = sums_ref[o // half, at] + term
         return carry
 
     lax.fori_loop(0, (n + CHUNK - 1) // CHUNK, step, 0)
@@ -88,22 +86,29 @@
     out_ref[:, each:] = jnp.broadcast_to(power, (parts, SUB, width))
 
 
-def bwd_kernel(cnt_ref, bp_ref, bo_ref, v_ref, jac_hbm, out_ref, acc, jac_ref, jsems):
-    n = cnt_ref[0, 0]
-    chunk = fetch(n, jac_hbm, jac_ref, jsems)
+def bwd_kernel(cnt, bp, bo, v_ref, jac, out_ref, acc):
+    width = jac.shape[1]
+    probes = v_ref.shape[1]
+    n = cnt[0, 0]
     acc[...] = jnp.zeros_like(acc)
 
     def step(c, carry):
-        chunk(c).wait()
-        for j in range(CHUNK):
-            s = c * CHUNK + j
-            v = v_ref[bo_ref[0, s]]
-            v = jnp.where(s < n, v, jnp.zeros_like(v))
-            term = lax.dot_general(
-                v, jac_ref[s], (((1,), (1,)), ((), ())), preferred_element_type=jnp.float32
+        for j in range(0, CHUNK, 2):
+            first = c * CHUNK + j
+            pair = []
+            for s in (first, first + 1):
+                v = v_ref[bo[0, s]]
+                pair.append(jnp.where(s < n, v, jnp.zeros_like(v)))
+            blocks = jac[pl.ds(first, 2)].reshape(2 * width, width)
+            terms = lax.dot_general(
+                jnp.concatenate(pair, axis=0),
+                blocks,
+                (((1,), (1,)), ((), ())),
+                preferred_element_type=jnp.float32,
             )
-            p = bp_ref[0, s]
-            acc[p] = acc[p] + term
+            for i in range(2):
+                p = bp[0, first + i]
+                acc[p] = acc[p] + terms[i * probes : (i + 1) * probes, i * width : (i + 1) * width]
         return carry
 
     lax.fori_loop(0, (n + CHUNK - 1) // CHUNK, step, 0)
@@ -121,8 +126,6 @@
     hbm = pl.BlockSpec(memory_space=pltpu.HBM)
     little = pltpu.CompilerParams(vmem_limit_bytes=8 << 20)
     params = pltpu.CompilerParams(vmem_limit_bytes=24 << 20)
-    blocks = pltpu.VMEM((slots, width, width), jac_blocks.dtype)
-    done = pltpu.SemaphoreType.DMA((slots // CHUNK,))
     held = [
         pltpu.with_memory_space_constraint(a, pltpu.HBM)
         for a in (block_param, block_obs, omega, jac_blocks)
@@ -136,20 +139,20 @@
         ((quarter * nz + lax.axis_index("z")) * per, 0, 0),
         (per, 1, width),
     )
-    sums, bp, bo = pl.pallas_call(
+    sums, jac, bp, bo = pl.pallas_call(
         fwd_kernel,
         out_shape=(
             jax.ShapeDtypeStruct((ncore, rows + SUB, width), jnp.float32),
+            jax.ShapeDtypeStruct((slots, width, width), jac_blocks.dtype),
             jax.ShapeDtypeStruct(block_param.shape, jnp.int32),
             jax.ShapeDtypeStruct(block_obs.shape, jnp.int32),
         ),
         in_specs=[smem] * 2 + [hbm] * 4,
-        out_specs=(vmem, smem, smem),
+        out_specs=(vmem, vmem, smem, smem),
         scratch_shapes=[
-            blocks,
             pltpu.VMEM(omega.shape, omega.dtype),
             pltpu.SemaphoreType.DMA((3,)),
-            done,
+            pltpu.SemaphoreType.DMA((slots // CHUNK,)),
         ],
         compiler_params=params,
         name="fwd_blocks",
@@ -191,12 +194,12 @@
     local_terms = pl.pallas_call(
         bwd_kernel,
         out_shape=jax.ShapeDtypeStruct((pblocks, probes, width), jnp.bfloat16),
-        in_specs=[smem, smem, smem, vmem, hbm],
+        in_specs=[smem, smem, smem, vmem, vmem],
         out_specs=vmem,
-        scratch_shapes=[pltpu.VMEM((pblocks, probes, width), jnp.float32), blocks, done],
+        scratch_shapes=[pltpu.VMEM((pblocks, probes, width), jnp.float32)],
         compiler_params=params,
         name="bwd_blocks",
-    )(block_count, bp, bo, scaled, held[3])
+    )(block_count, bp, bo, scaled, jac)
 
     n = lax.axis_size(GRP)
     got = lax.all_to_all(local_terms, GRP, 0, 0, tiled=True)

time: 95.2 us -> 92.3 us (0.970)
  blocking collectives: 68.2 us -> 66.6 us
    all_to_all x1, blocking collectives: 14.2 us -> 13 us  [on_device(): got = lax.all_to_all(local_terms, GRP, 0, 0, tiled=True)]
    pallas_call x1, Pallas kernels: 2.49 us -> 1.53 us  [on_device(): pl.pallas_call(bwd_kernel, out_shape=jax.ShapeDtypeStruct((pblocks, probe...]
where the time goes in v5:
time: 92.3 us; the launch traced here: 91.5 us
  blocking collectives  66.6 us (72%)
  starting transfers between devices  10.7 us (12%)
  waiting for transfers between devices  7.74 us (8%)
  Pallas kernels  4.73 us (5%)
    all_to_all x1, blocking collectives, on_device(): got = lax.all_to_all(packed.astype(jnp.float16), 'z', 0, 0, tiled=True)  21.8 us
    all_to_all x1, blocking collectives, on_device(): scaled = lax.all_to_all(scaled, 'z', 0, 0, tiled=True)  19.3 us
    all_to_all x1, blocking collectives, on_device(): got = lax.all_to_all(local_terms, GRP, 0, 0, tiled=True)  13 us
    ppermute x1, starting transfers between devices, on_device(): lax.ppermute(sums[1], 'core', swap)  8.79 us
    all_gather x1, blocking collectives, on_device(): scaled = lax.all_gather(scaled, 'core', axis=0, tiled=True)  6.52 us
    ppermute x1, waiting for transfers between devices, on_device(): lax.ppermute(other.astype(jnp.float16), 'yh', swap).astype(jnp.float32)  6.22 us
    all_gather x1, blocking collectives, on_device(): scaled = lax.all_gather(scaled, 'yh', axis=0, tiled=True)  5.99 us
    pallas_call x1, Pallas kernels, on_device(): pl.pallas_call(fwd_kernel, out_shape=(jax.ShapeDtypeStruct((ncore, rows +...  3.08 us
  transfers between devices with their start and end apart: 2, of which 2 were waited for; matrix products, arithmetic and copies ran while one was open for 0% of the time, Pallas kernels for 0%

profile of v5, /device:TPU:1, one launch (start us, length us, event | category | flops | bytes accessed | tf_op | source)
XLA Modules:
  0.0 91.5 jit_solution(7107761029597171490)
XLA Ops:
  0.0 0.0 copy-start
  0.7 0.1 copy-done
  0.8 3.1 %fwd_blocks.1 = (f32[2,1032,128]{2,1,0:T(8,128)S(1)}, bf16[128,128,128]{2,1,0:T(8,128)(2,1)S(1)}, s32[1,128]{1,0:T(1,128)S(1)}, s32[1,128]{1,0:T(1,128)S(1)}) custom-call(s32[1,1]{1,0:T(1,128)} %bitcast.me, s32[1,1]{1,0:T(1,128)S(6)} %copy.13.cnt, s32[1,128]{1,0:T(1,128)} %bp_hbm.1, s32[1,128]{1,0:T(1,128)} %bo_hbm.1, bf16[32,8192]{1,0:T(8,128)(2,1)} %omega_hbm.1, ...), custom_call_target="tpu_custom_call" | custom-call | tf_op jit(solution)/shard_map/fwd_blocks/pallas_call | solution.py:142
  3.9 8.8 %collective-permute-start = (f32[1032,128]{1,0:T(8,128)S(1)}, f32[1032,128]{1,0:T(8,128)S(1)}, u32[]{:S(2)}, u32[]{:S(2)}) collective-permute-start(f32[1032,128]{1,0:T(8,128)S(1)} %slice_bitcast_fusion), channel_id=1, source_target_pairs={{0,1},{1,0},{2,3},{3,2},{4,5},{5,4},{6,7},{7,6},{8,9},{9,8},{10,11... | collective-permute-start | bytes 1585160 | tf_op jit(solution)/shard_map/ppermute | solution.py:173
  12.7 1.5 %collective-permute-done.got_ref = f32[1032,128]{1,0:T(8,128)S(1)} collective-permute-done((f32[1032,128]{1,0:T(8,128)S(1)}, f32[1032,128]{1,0:T(8,128)S(1)}, u32[]{:S(2)}, u32[]{:S(2)}) %collective-permute-start) | collective-permute-done | bytes 528416 | tf_op jit(solution)/shard_map/ppermute | solution.py:173
  14.2 0.1 add_core.1
  14.3 1.9 %collective-permute-start.1 = (f16[520,128]{1,0:T(8,128)(2,1)S(1)}, f16[520,128]{1,0:T(8,128)(2,1)S(1)}, u32[]{:S(2)}, u32[]{:S(2)}) collective-permute-start(f16[520,128]{1,0:T(8,128)(2,1)S(1)} %convert_element_type.27), channel_id=1, source_target_pairs={{0,2},{2,0},{1,3},{3,1},{4,6},{6,4},{5,7},{7,5},{8,10},{10,8},{9,1... | collective-permute-start | bytes 399368 | tf_op jit(solution)/shard_map/ppermute | solution.py:174
  16.3 6.2 %collective-permute-done.1 = f16[520,128]{1,0:T(8,128)(2,1)S(1)} collective-permute-done((f16[520,128]{1,0:T(8,128)(2,1)S(1)}, f16[520,128]{1,0:T(8,128)(2,1)S(1)}, u32[]{:S(2)}, u32[]{:S(2)}) %collective-permute-start.1) | collective-permute-done | bytes 133152 | tf_op jit(solution)/shard_map/ppermute | solution.py:174
  22.5 0.1 add_chip.1
  22.6 21.8 %all_to_all.15 = f16[16,40,128]{2,1,0:T(8,128)(2,1)S(1)} all-to-all(f16[16,40,128]{2,1,0:T(8,128)(2,1)S(1)} %convert_element_type.29), channel_id=1, replica_groups=mesh['x'=4,'yl'=2,'z'=16,'yh'=2,'core'=2] {'z'}, dimensions={0} | all-to-all | bytes 327680 | tf_op jit(solution)/shard_map/all_to_all | solution.py:183
  44.5 19.3 %all_to_all.16 = bf16[16,32,128]{2,1,0:T(8,128)(2,1)S(1)} all-to-all(bf16[16,32,128]{2,1,0:T(8,128)(2,1)S(1)} %reshape.42), channel_id=1, replica_groups=mesh['x'=4,'yl'=2,'z'=16,'yh'=2,'core'=2] {'z'}, dimensions={0} | all-to-all | bytes 262144 | tf_op jit(solution)/shard_map/all_to_all | solution.py:190
  63.8 6.0 %all_gather.6 = bf16[32,32,128]{2,1,0:T(8,128)(2,1)S(1)} all-gather(bf16[16,32,128]{2,1,0:T(8,128)(2,1)S(1)} %all_to_all.16), channel_id=1, replica_groups=mesh['x'=4,'yl'=2,'z'=16,'yh'=2,'core'=2] {'yh'}, dimensions={0}, use_global_device_ids=true | all-gather | bytes 393216 | tf_op jit(solution)/shard_map/all_gather | solution.py:191
  69.8 6.5 %all_gather.7.v_ref = bf16[64,32,128]{2,1,0:T(8,128)(2,1)S(1)} all-gather(bf16[32,32,128]{2,1,0:T(8,128)(2,1)S(1)} %all_gather.6), channel_id=1, replica_groups=mesh['x'=4,'yl'=2,'z'=16,'yh'=2,'core'=2] {'core'}, dimensions={0}, use_global_device_ids=true | all-gather | bytes 786432 | tf_op jit(solution)/shard_map/all_gather | solution.py:192
  76.3 1.5 %bwd_blocks.1 = bf16[64,32,128]{2,1,0:T(8,128)(2,1)S(1)} custom-call(s32[1,1]{1,0:T(1,128)S(6)} %copy.13.cnt, s32[1,128]{1,0:T(1,128)S(1)} %get-tuple-element.13.bp, s32[1,128]{1,0:T(1,128)S(1)} %get-tuple-element.14.bo, bf16[64,32,128]{2,1,0:T(8,128)(2,1)S(1)} %all_gather.7.v_ref, bf16[128,128,128]{2,1,0:T(8,128)(2,1)S(1)} %get-tuple-element.20.jac), custom_call_target="tpu_custom_call" | custom-call | tf_op jit(solution)/shard_map/bwd_blocks/pallas_call | solution.py:194
  77.8 13.0 %all_to_all.17 = bf16[64,32,128]{2,1,0:T(8,128)(2,1)S(1)} all-to-all(bf16[64,32,128]{2,1,0:T(8,128)(2,1)S(1)} %bwd_blocks.1), channel_id=1, replica_groups=mesh['x'=4,'yl'=2,'z'=16,'yh'=2,'core'=2] {'x','yl'}, dimensions={0} | all-to-all | bytes 1048576 | tf_op jit(solution)/shard_map/all_to_all | solution.py:205
  90.8 0.1 convert_reduce_fusion
  90.9 0.7 copy_bitcast_fusion
  (9 shorter events, 0.2 us)
Async XLA Ops:
  0.0 0.8 copy-start
  3.9 10.3 %collective-permute-start = (f32[1032,128]{1,0:T(8,128)S(1)}, f32[1032,128]{1,0:T(8,128)S(1)}, u32[]{:S(2)}, u32[]{:S(2)}) collective-permute-start(f32[1032,128]{1,0:T(8,128)S(1)} %slice_bitcast_fusion), channel_id=1, source_target_pairs={{0,1},{1,0},{2,3},{3,2},{4,5},{5,4},{6,7},{7,6},{8,9},{9,8},{10,11... | collective-permute-start | bytes 1585160 | tf_op jit(solution)/shard_map/ppermute | solution.py:173
  14.3 8.2 %collective-permute-start.1 = (f16[520,128]{1,0:T(8,128)(2,1)S(1)}, f16[520,128]{1,0:T(8,128)(2,1)S(1)}, u32[]{:S(2)}, u32[]{:S(2)}) collective-permute-start(f16[520,128]{1,0:T(8,128)(2,1)S(1)} %convert_element_type.27), channel_id=1, source_target_pairs={{0,2},{2,0},{1,3},{3,1},{4,6},{6,4},{5,7},{7,5},{8,10},{10,8},{9,1... | collective-permute-start | bytes 399368 | tf_op jit(solution)/shard_map/ppermute | solution.py:174

commit v6 on v5

--- a/solution.py
+++ b/solution.py
@@ -7,7 +7,8 @@
 
 CHUNK = 64
 SUB = 8
-PAR = ("z", "yh", "core")
+PAR = ("zh", "zl", "yh", "core")
+NEAR = ("zl", "yh")
 GRP = ("x", "yl")
 
 
@@ -37,7 +38,7 @@
             chunk(c).start()
 
     sums_ref[...] = jnp.zeros_like(sums_ref)
-    flip = me[0, 0] * (half // 2)
+    flip = me[0, 0] * half
     for copy in small:
         copy.wait()
 
@@ -62,28 +63,45 @@
         sums_ref[i, rows:] = top
 
 
-def core_kernel(sums_ref, got_ref, mine_ref, other_ref):
-    half = mine_ref.shape[0]
-    width = mine_ref.shape[1]
-    top = sums_ref[0, 2 * half :] + got_ref[2 * half :]
-    power = jnp.clip(jnp.ceil(jnp.log2(top)), -100.0, 100.0) - 14.0
-    mine_ref[...] = sums_ref[0, :half] + got_ref[:half]
-    other = sums_ref[0, half : 2 * half] + got_ref[half : 2 * half]
-    other = other.reshape(half // SUB, SUB, width) * jnp.exp2(-power)
-    other_ref[:half] = other.reshape(half, width)
-    other_ref[half:] = power
-
-
-def chip_kernel(mine_ref, sent_ref, got_ref, out_ref):
+def exponent(top):
+    return jnp.clip(jnp.ceil(jnp.log2(top)), -100.0, 100.0) - 14.0
+
+
+def unscaled_sum(got_ref):
+    parts, each, width = got_ref.shape
+    each = each - SUB
+    total = None
+    for i in range(parts):
+        data = got_ref[i, :each].reshape(each // SUB, SUB, width) * jnp.exp2(got_ref[i, each:])
+        total = data if total is None else total + data
+    return total
+
+
+def core_kernel(sums_ref, got_ref, out_ref):
     parts, each, width = out_ref.shape
     each = each - SUB
-    half = mine_ref.shape[0]
-    theirs = got_ref[half:]
-    power = jnp.maximum(sent_ref[half:], theirs) + 1.0
-    got = got_ref[:half].reshape(half // SUB, SUB, width) * jnp.exp2(theirs - power)
-    data = mine_ref[...].reshape(half // SUB, SUB, width) * jnp.exp2(-power) + got
+    rows = parts * each
+    power = exponent(sums_ref[0, rows:] + got_ref[rows:])
+    data = (sums_ref[0, :rows] + got_ref[:rows]).reshape(rows // SUB, SUB, width) * jnp.exp2(-power)
     out_ref[:, :each] = data.reshape(parts, each, width)
     out_ref[:, each:] = jnp.broadcast_to(power, (parts, SUB, width))
+
+
+def near_kernel(got_ref, out_ref):
+    rows, width = out_ref.shape
+    rows = rows - SUB
+    total = unscaled_sum(got_ref)
+    power = exponent(jnp.max(jnp.abs(total), axis=0))
+    out_ref[:rows] = (total * jnp.exp2(-power)).reshape(rows, width)
+    out_ref[rows:] = power
+
+
+def far_kernel(got_ref, weight_ref, out_ref):
+    copies, rows, width = out_ref.shape
+    per = weight_ref.shape[0]
+    total = unscaled_sum(got_ref).reshape(per, rows // per, width)
+    scaled = (total * weight_ref[...]).reshape(rows, width).astype(out_ref.dtype)
+    out_ref[...] = jnp.broadcast_to(scaled, (copies, rows, width))
 
 
 def bwd_kernel(cnt, bp, bo, v_ref, jac, out_ref, acc):
@@ -120,7 +138,7 @@
     slots, width = jac_blocks.shape[1], jac_blocks.shape[2]
     pblocks = omega.shape[1] // width
     oblocks = obs_weight.shape[1] // width
-    nz, nyh, ncore = (lax.axis_size(a) for a in PAR)
+    ncore, nnear = lax.axis_size("core"), lax.axis_size(NEAR)
     smem = pl.BlockSpec(memory_space=pltpu.SMEM)
     vmem = pl.BlockSpec(memory_space=pltpu.VMEM)
     hbm = pl.BlockSpec(memory_space=pltpu.HBM)
@@ -131,14 +149,10 @@
         for a in (block_param, block_obs, omega, jac_blocks)
     ]
     rows = oblocks // ncore * probes
-    each = oblocks // (nz * nyh * ncore) * probes
+    each = rows // nnear
     per = each // probes
-    quarter = lax.axis_index("core") * nyh + lax.axis_index("yh")
-    weight = lax.dynamic_slice(
-        obs_weight.reshape(oblocks, 1, width),
-        ((quarter * nz + lax.axis_index("z")) * per, 0, 0),
-        (per, 1, width),
-    )
+    first = (lax.axis_index("core") * nnear + lax.axis_index(NEAR)) * per
+    weight = lax.dynamic_slice(obs_weight.reshape(oblocks, 1, width), (first, 0, 0), (per, 1, width))
     sums, jac, bp, bo = pl.pallas_call(
         fwd_kernel,
         out_shape=(
@@ -156,40 +170,27 @@
         ],
         compiler_params=params,
         name="fwd_blocks",
-    )(quarter.reshape(1, 1), block_count, *held)
+    )(lax.axis_index("core").reshape(1, 1), block_count, *held)
     sums, weight = lax.optimization_barrier((sums, weight))
 
-    swap = [(i, 1 - i) for i in range(2)]
-    mine, other = pl.pallas_call(
-        core_kernel,
-        out_shape=(
-            jax.ShapeDtypeStruct((rows // nyh, width), jnp.float32),
-            jax.ShapeDtypeStruct((rows // nyh + SUB, width), jnp.float32),
-        ),
-        in_specs=[vmem] * 2,
-        out_specs=(vmem, vmem),
-        compiler_params=little,
-        name="add_core",
-    )(sums, lax.ppermute(sums[1], "core", swap))
-    got = lax.ppermute(other.astype(jnp.float16), "yh", swap).astype(jnp.float32)
-    packed = pl.pallas_call(
-        chip_kernel,
-        out_shape=jax.ShapeDtypeStruct((nz, each + SUB, width), jnp.float32),
-        in_specs=[vmem] * 3,
-        out_specs=vmem,
-        compiler_params=little,
-        name="add_chip",
-    )(mine, other, got)
-    got = lax.all_to_all(packed.astype(jnp.float16), "z", 0, 0, tiled=True)
-    scale = jnp.exp2(got[:, each:].astype(jnp.float32))
-    data = got[:, :each].astype(jnp.float32).reshape(nz, each // SUB, SUB, width)
-    owned = jnp.sum(data * scale[:, None], axis=0).reshape(per, probes, width)
-
-    scaled = (owned * weight).astype(jnp.bfloat16)
-    scaled = jnp.broadcast_to(scaled, (nz, per, probes, width)).reshape(nz * per, probes, width)
-    scaled = lax.all_to_all(scaled, "z", 0, 0, tiled=True)
-    scaled = lax.all_gather(scaled, "yh", axis=0, tiled=True)
-    scaled = lax.all_gather(scaled, "core", axis=0, tiled=True)
+    def small_call(kernel, shape, dtype, name):
+        return pl.pallas_call(
+            kernel,
+            out_shape=jax.ShapeDtypeStruct(shape, dtype),
+            out_specs=vmem,
+            compiler_params=little,
+            name=name,
+        )
+
+    packed = small_call(core_kernel, (nnear, each + SUB, width), jnp.float32, "add_core")(
+        sums, lax.ppermute(sums[1], "core", [(0, 1), (1, 0)])
+    )
+    got = lax.all_to_all(packed.astype(jnp.float16), NEAR, 0, 0, tiled=True).astype(jnp.float32)
+    packed = small_call(near_kernel, (each + SUB, width), jnp.float32, "add_near")(got)
+    got = lax.all_gather(packed.astype(jnp.float16), "zh").astype(jnp.float32)
+    scaled = small_call(far_kernel, (nnear, each, width), jnp.bfloat16, "add_far")(got, weight)
+    scaled = lax.all_to_all(scaled, NEAR, 0, 0, tiled=True).reshape(rows, width)
+    scaled = lax.all_gather(scaled, "core", axis=0, tiled=True).reshape(oblocks, probes, width)
 
     local_terms = pl.pallas_call(
         bwd_kernel,
@@ -209,7 +210,7 @@
 
 
 def solution(mesh):
-    mesh = Mesh(mesh.devices.reshape(4, 2, 16, 2, 2), GRP + PAR)
+    mesh = Mesh(mesh.devices.reshape(4, 2, 4, 4, 2, 2), GRP + PAR)
     in_specs = (
         P(None, PAR),
         P(GRP, PAR, None, None),

time: 92.3 us -> 83.4 us (0.904)
  waiting for transfers between devices: 7.74 us -> 1.52 us
  starting transfers between devices: 10.7 us -> 8.79 us
    all_to_all x2, blocking collectives: 41.1 us -> 25.8 us  [the longest x1 13 us: on_device(): scaled = lax.all_to_all(scaled, NEAR, 0, 0, tiled=True).reshape(rows, width)]
    all_gather x2, blocking collectives: 12.5 us -> 27.5 us  [the longest x1 20.9 us: on_device(): got = lax.all_gather(packed.astype(jnp.float16), 'zh').astype(jnp.float32)]
    ppermute x2 -> x1, waiting for transfers between devices: 7.74 us -> 1.52 us  [on_device(): lax.ppermute(sums[1], 'core', [(0, 1), (1, 0)])]
    ppermute x2 -> x1, starting transfers between devices: 10.7 us -> 8.79 us  [on_device(): lax.ppermute(sums[1], 'core', [(0, 1), (1, 0)])]
  transfers between devices with their start and end apart: 2 -> 1, of which waited for: 2 -> 1; matrix products, arithmetic and copies ran while one was open for 0% -> 0% of each run, Pallas kernels for 0% -> 0%
where the time goes in v6:
time: 83.4 us; the launch traced here: 82.9 us
  blocking collectives  66.1 us (79%)
  starting transfers between devices  8.79 us (11%)
  Pallas kernels  4.76 us (6%)
  waiting for transfers between devices  1.52 us (2%)
    all_gather x1, blocking collectives, on_device(): got = lax.all_gather(packed.astype(jnp.float16), 'zh').astype(jnp.float32)  20.9 us
    all_to_all x1, blocking collectives, on_device(): scaled = lax.all_to_all(scaled, NEAR, 0, 0, tiled=True).reshape(rows, width)  13 us
    all_to_all x1, blocking collectives, on_device(): got = lax.all_to_all(local_terms, GRP, 0, 0, tiled=True)  12.9 us
    all_to_all x1, blocking collectives, on_device(): lax.all_to_all(packed.astype(jnp.float16), NEAR, 0, 0, tiled=True)  12.8 us
    ppermute x1, starting transfers between devices, on_device(): lax.ppermute(sums[1], 'core', [(0, 1), (1, 0)])  8.79 us
    all_gather x1, blocking collectives, on_device(): lax.all_gather(scaled, 'core', axis=0, tiled=True)  6.58 us
    pallas_call x1, Pallas kernels, on_device(): pl.pallas_call(fwd_kernel, out_shape=(jax.ShapeDtypeStruct((ncore, rows +...  3.08 us
  transfers between devices with their start and end apart: 1, of which 1 were waited for; matrix products, arithmetic and copies ran while one was open for 0% of the time, Pallas kernels for 0%

profile of v6, /device:TPU:1, one launch (start us, length us, event | category | flops | bytes accessed | tf_op | source)
XLA Modules:
  0.0 82.9 jit_solution(720398076955118374)
XLA Ops:
  0.0 0.0 copy-start
  0.7 0.1 copy-done
  0.8 3.1 %fwd_blocks.1 = (f32[2,1032,128]{2,1,0:T(8,128)S(1)}, bf16[128,128,128]{2,1,0:T(8,128)(2,1)S(1)}, s32[1,128]{1,0:T(1,128)S(1)}, s32[1,128]{1,0:T(1,128)S(1)}) custom-call(s32[1,1]{1,0:T(1,128)} %bitcast.me, s32[1,1]{1,0:T(1,128)S(6)} %copy.10.cnt, s32[1,128]{1,0:T(1,128)} %bp_hbm.1, s32[1,128]{1,0:T(1,128)} %bo_hbm.1, bf16[32,8192]{1,0:T(8,128)(2,1)} %omega_hbm.1, ...), custom_call_target="tpu_custom_call" | custom-call | tf_op jit(solution)/shard_map/fwd_blocks/pallas_call | solution.py:156
  3.9 8.8 %collective-permute-start = (f32[1032,128]{1,0:T(8,128)S(1)}, f32[1032,128]{1,0:T(8,128)S(1)}, u32[]{:S(2)}, u32[]{:S(2)}) collective-permute-start(f32[1032,128]{1,0:T(8,128)S(1)} %slice_bitcast_fusion), channel_id=1, source_target_pairs={{0,1},{1,0},{2,3},{3,2},{4,5},{5,4},{6,7},{7,6},{8,9},{9,8},{10,11... | collective-permute-start | bytes 1585160 | tf_op jit(solution)/shard_map/ppermute | solution.py:186
  12.7 1.5 %collective-permute-done.got_ref = f32[1032,128]{1,0:T(8,128)S(1)} collective-permute-done((f32[1032,128]{1,0:T(8,128)S(1)}, f32[1032,128]{1,0:T(8,128)S(1)}, u32[]{:S(2)}, u32[]{:S(2)}) %collective-permute-start) | collective-permute-done | bytes 528416 | tf_op jit(solution)/shard_map/ppermute | solution.py:186
  14.2 0.1 add_core.1
  14.3 12.8 %all_to_all.15 = f16[8,136,128]{2,1,0:T(8,128)(2,1)S(1)} all-to-all(f16[8,136,128]{2,1,0:T(8,128)(2,1)S(1)} %convert_element_type.18), channel_id=1, replica_groups=mesh['x'=4,'yl'=2,'zh'=4,'zl'=4,'yh'=2,'core'=2] {'zl','yh'}, dimensions={0} | all-to-all | bytes 557056 | tf_op jit(solution)/shard_map/all_to_all | solution.py:188
  27.2 0.1 add_near.1
  27.3 20.9 %all-gather = f16[544,128]{1,0:T(8,128)(2,1)S(1)} all-gather(f16[136,128]{1,0:T(8,128)(2,1)S(1)} %convert_element_type.20), channel_id=2, replica_groups=mesh['x'=4,'yl'=2,'zh'=4,'zl'=4,'yh'=2,'core'=2] {'zh'}, dimensions={0}, use_global_device_ids=true | all-gather | bytes 174080 | tf_op jit(solution)/shard_map/all_gather | solution.py:190
  48.2 13.0 %all_to_all.16 = bf16[8,128,128]{2,1,0:T(8,128)(2,1)S(1)} all-to-all(bf16[8,128,128]{2,1,0:T(8,128)(2,1)S(1)} %add_far.1), channel_id=1, replica_groups=mesh['x'=4,'yl'=2,'zh'=4,'zl'=4,'yh'=2,'core'=2] {'zl','yh'}, dimensions={0} | all-to-all | bytes 524288 | tf_op jit(solution)/shard_map/all_to_all | solution.py:192
  61.2 6.6 %all_gather.11 = bf16[2048,128]{1,0:T(8,128)(2,1)S(1)} all-gather(bf16[1024,128]{1,0:T(8,128)(2,1)S(1)} %bitcast.19), channel_id=1, replica_groups=mesh['x'=4,'yl'=2,'zh'=4,'zl'=4,'yh'=2,'core'=2] {'core'}, dimensions={0}, use_global_device_ids=true | all-gather | bytes 786432 | tf_op jit(solution)/shard_map/all_gather | solution.py:193
  67.8 1.5 %bwd_blocks.1 = bf16[64,32,128]{2,1,0:T(8,128)(2,1)S(1)} custom-call(s32[1,1]{1,0:T(1,128)S(6)} %copy.10.cnt, s32[1,128]{1,0:T(1,128)S(1)} %get-tuple-element.11.bp, s32[1,128]{1,0:T(1,128)S(1)} %get-tuple-element.12.bo, bf16[64,32,128]{2,1,0:T(8,128)(2,1)S(1)} %bitcast.17, bf16[128,128,128]{2,1,0:T(8,128)(2,1)S(1)} %get-tuple-element.16.jac), custom_call_target="tpu_custom_call" | custom-call | tf_op jit(solution)/shard_map/bwd_blocks/pallas_call | solution.py:195
  69.3 12.9 %all_to_all.17 = bf16[64,32,128]{2,1,0:T(8,128)(2,1)S(1)} all-to-all(bf16[64,32,128]{2,1,0:T(8,128)(2,1)S(1)} %bwd_blocks.1), channel_id=1, replica_groups=mesh['x'=4,'yl'=2,'zh'=4,'zl'=4,'yh'=2,'core'=2] {'x','yl'}, dimensions={0} | all-to-all | bytes 1048576 | tf_op jit(solution)/shard_map/all_to_all | solution.py:206
  82.1 0.1 convert_reduce_fusion
  82.2 0.7 copy_bitcast_fusion
  (7 shorter events, 0.2 us)
Async XLA Ops:
  0.0 0.8 copy-start
  3.9 10.3 %collective-permute-start = (f32[1032,128]{1,0:T(8,128)S(1)}, f32[1032,128]{1,0:T(8,128)S(1)}, u32[]{:S(2)}, u32[]{:S(2)}) collective-permute-start(f32[1032,128]{1,0:T(8,128)S(1)} %slice_bitcast_fusion), channel_id=1, source_target_pairs={{0,1},{1,0},{2,3},{3,2},{4,5},{5,4},{6,7},{7,6},{8,9},{9,8},{10,11... | collective-permute-start | bytes 1585160 | tf_op jit(solution)/shard_map/ppermute | solution.py:186

commit v7 on v6

--- a/solution.py
+++ b/solution.py
@@ -187,7 +187,9 @@
     )
     got = lax.all_to_all(packed.astype(jnp.float16), NEAR, 0, 0, tiled=True).astype(jnp.float32)
     packed = small_call(near_kernel, (each + SUB, width), jnp.float32, "add_near")(got)
-    got = lax.all_gather(packed.astype(jnp.float16), "zh").astype(jnp.float32)
+    nfar = lax.axis_size("zh")
+    copies = jnp.broadcast_to(packed.astype(jnp.float16), (nfar,) + packed.shape)
+    got = lax.all_to_all(copies, "zh", 0, 0, tiled=True).astype(jnp.float32)
     scaled = small_call(far_kernel, (nnear, each, width), jnp.bfloat16, "add_far")(got, weight)
     scaled = lax.all_to_all(scaled, NEAR, 0, 0, tiled=True).reshape(rows, width)
     scaled = lax.all_gather(scaled, "core", axis=0, tiled=True).reshape(oblocks, probes, width)

time: 83.4 us -> 86.8 us (1.041)
  blocking collectives: 66.1 us -> 69.4 us
    all_to_all x0 -> x1, blocking collectives: none -> 25.5 us  [on_device(): got = lax.all_to_all(copies, 'zh', 0, 0, tiled=True).astype(jnp.float32)]
    all_gather x1 -> x0, blocking collectives: 20.9 us -> none  [on_device(): got = lax.all_gather(packed.astype(jnp.float16), 'zh').astype(jnp.float32)]
    all_to_all x1, blocking collectives: 13 us -> 11 us  [on_device(): scaled = lax.all_to_all(scaled, NEAR, 0, 0, tiled=True).reshape(rows, width)]
where the time goes in v7:
time: 86.8 us; the launch traced here: 86.2 us
  blocking collectives  69.4 us (80%)
  starting transfers between devices  8.79 us (10%)
  Pallas kernels  4.75 us (5%)
  waiting for transfers between devices  1.52 us (2%)
    all_to_all x1, blocking collectives, on_device(): got = lax.all_to_all(copies, 'zh', 0, 0, tiled=True).astype(jnp.float32)  25.5 us
    all_to_all x1, blocking collectives, on_device(): lax.all_to_all(packed.astype(jnp.float16), NEAR, 0, 0, tiled=True)  13.6 us
    all_to_all x1, blocking collectives, on_device(): got = lax.all_to_all(local_terms, GRP, 0, 0, tiled=True)  12.6 us
    all_to_all x1, blocking collectives, on_device(): scaled = lax.all_to_all(scaled, NEAR, 0, 0, tiled=True).reshape(rows, width)  11 us
    ppermute x1, starting transfers between devices, on_device(): lax.ppermute(sums[1], 'core', [(0, 1), (1, 0)])  8.79 us
    all_gather x1, blocking collectives, on_device(): lax.all_gather(scaled, 'core', axis=0, tiled=True)  6.74 us
    pallas_call x1, Pallas kernels, on_device(): pl.pallas_call(fwd_kernel, out_shape=(jax.ShapeDtypeStruct((ncore, rows +...  3.07 us
  transfers between devices with their start and end apart: 1, of which 1 were waited for; matrix products, arithmetic and copies ran while one was open for 0% of the time, Pallas kernels for 0%

profile of v7, /device:TPU:1, one launch (start us, length us, event | category | flops | bytes accessed | tf_op | source)
XLA Modules:
  0.0 86.2 jit_solution(14374321992775669602)
XLA Ops:
  0.0 0.0 copy-start
  0.7 0.1 copy-done
  0.8 3.1 %fwd_blocks.1 = (f32[2,1032,128]{2,1,0:T(8,128)S(1)}, bf16[128,128,128]{2,1,0:T(8,128)(2,1)S(1)}, s32[1,128]{1,0:T(1,128)S(1)}, s32[1,128]{1,0:T(1,128)S(1)}) custom-call(s32[1,1]{1,0:T(1,128)} %bitcast.me, s32[1,1]{1,0:T(1,128)S(6)} %copy.10.cnt, s32[1,128]{1,0:T(1,128)} %bp_hbm.1, s32[1,128]{1,0:T(1,128)} %bo_hbm.1, bf16[32,8192]{1,0:T(8,128)(2,1)} %omega_hbm.1, ...), custom_call_target="tpu_custom_call" | custom-call | tf_op jit(solution)/shard_map/fwd_blocks/pallas_call | solution.py:156
  3.9 8.8 %collective-permute-start = (f32[1032,128]{1,0:T(8,128)S(1)}, f32[1032,128]{1,0:T(8,128)S(1)}, u32[]{:S(2)}, u32[]{:S(2)}) collective-permute-start(f32[1032,128]{1,0:T(8,128)S(1)} %slice_bitcast_fusion), channel_id=1, source_target_pairs={{0,1},{1,0},{2,3},{3,2},{4,5},{5,4},{6,7},{7,6},{8,9},{9,8},{10,11... | collective-permute-start | bytes 1585160 | tf_op jit(solution)/shard_map/ppermute | solution.py:186
  12.7 1.5 %collective-permute-done.got_ref = f32[1032,128]{1,0:T(8,128)S(1)} collective-permute-done((f32[1032,128]{1,0:T(8,128)S(1)}, f32[1032,128]{1,0:T(8,128)S(1)}, u32[]{:S(2)}, u32[]{:S(2)}) %collective-permute-start) | collective-permute-done | bytes 528416 | tf_op jit(solution)/shard_map/ppermute | solution.py:186
  14.2 0.1 add_core.1
  14.3 13.6 %all_to_all.20 = f16[8,136,128]{2,1,0:T(8,128)(2,1)S(1)} all-to-all(f16[8,136,128]{2,1,0:T(8,128)(2,1)S(1)} %convert_element_type.18), channel_id=1, replica_groups=mesh['x'=4,'yl'=2,'zh'=4,'zl'=4,'yh'=2,'core'=2] {'zl','yh'}, dimensions={0} | all-to-all | bytes 557056 | tf_op jit(solution)/shard_map/all_to_all | solution.py:188
  27.9 0.1 add_near.1
  28.1 25.5 %all_to_all.21 = f16[4,136,128]{2,1,0:T(8,128)(2,1)S(1)} all-to-all(f16[4,136,128]{2,1,0:T(8,128)(2,1)S(1)} %broadcast_in_dim.3), channel_id=1, replica_groups=mesh['x'=4,'yl'=2,'zh'=4,'zl'=4,'yh'=2,'core'=2] {'zh'}, dimensions={0} | all-to-all | bytes 278528 | tf_op jit(solution)/shard_map/all_to_all | solution.py:192
  53.6 11.0 %all_to_all.22 = bf16[8,128,128]{2,1,0:T(8,128)(2,1)S(1)} all-to-all(bf16[8,128,128]{2,1,0:T(8,128)(2,1)S(1)} %add_far.1), channel_id=1, replica_groups=mesh['x'=4,'yl'=2,'zh'=4,'zl'=4,'yh'=2,'core'=2] {'zl','yh'}, dimensions={0} | all-to-all | bytes 524288 | tf_op jit(solution)/shard_map/all_to_all | solution.py:194
  64.6 6.7 %all_gather.3 = bf16[2048,128]{1,0:T(8,128)(2,1)S(1)} all-gather(bf16[1024,128]{1,0:T(8,128)(2,1)S(1)} %bitcast.17), channel_id=1, replica_groups=mesh['x'=4,'yl'=2,'zh'=4,'zl'=4,'yh'=2,'core'=2] {'core'}, dimensions={0}, use_global_device_ids=true | all-gather | bytes 786432 | tf_op jit(solution)/shard_map/all_gather | solution.py:195
  71.4 1.5 %bwd_blocks.1 = bf16[64,32,128]{2,1,0:T(8,128)(2,1)S(1)} custom-call(s32[1,1]{1,0:T(1,128)S(6)} %copy.10.cnt, s32[1,128]{1,0:T(1,128)S(1)} %get-tuple-element.11.bp, s32[1,128]{1,0:T(1,128)S(1)} %get-tuple-element.12.bo, bf16[64,32,128]{2,1,0:T(8,128)(2,1)S(1)} %bitcast.15, bf16[128,128,128]{2,1,0:T(8,128)(2,1)S(1)} %get-tuple-element.16.jac), custom_call_target="tpu_custom_call" | custom-call | tf_op jit(solution)/shard_map/bwd_blocks/pallas_call | solution.py:197
  72.9 12.6 %all_to_all.23 = bf16[64,32,128]{2,1,0:T(8,128)(2,1)S(1)} all-to-all(bf16[64,32,128]{2,1,0:T(8,128)(2,1)S(1)} %bwd_blocks.1), channel_id=1, replica_groups=mesh['x'=4,'yl'=2,'zh'=4,'zl'=4,'yh'=2,'core'=2] {'x','yl'}, dimensions={0} | all-to-all | bytes 1048576 | tf_op jit(solution)/shard_map/all_to_all | solution.py:208
  85.5 0.1 convert_reduce_fusion
  85.5 0.7 copy_bitcast_fusion
  (8 shorter events, 0.2 us)
Async XLA Ops:
  0.0 0.8 copy-start
  3.9 10.3 %collective-permute-start = (f32[1032,128]{1,0:T(8,128)S(1)}, f32[1032,128]{1,0:T(8,128)S(1)}, u32[]{:S(2)}, u32[]{:S(2)}) collective-permute-start(f32[1032,128]{1,0:T(8,128)S(1)} %slice_bitcast_fusion), channel_id=1, source_target_pairs={{0,1},{1,0},{2,3},{3,2},{4,5},{5,4},{6,7},{7,6},{8,9},{9,8},{10,11... | collective-permute-start | bytes 1585160 | tf_op jit(solution)/shard_map/ppermute | solution.py:186

commit v8 on v6

--- a/solution.py
+++ b/solution.py
@@ -10,6 +10,10 @@
 PAR = ("zh", "zl", "yh", "core")
 NEAR = ("zl", "yh")
 GRP = ("x", "yl")
+
+
+def exponent(top):
+    return jnp.clip(jnp.ceil(jnp.log2(top)), -100.0, 100.0) - 14.0
 
 
 def fwd_kernel(
@@ -59,12 +63,11 @@
     top = jnp.zeros((SUB, width), jnp.float32)
     for i in range(2):
         top = jnp.maximum(top, jnp.max(jnp.abs(sums_ref[i, :rows].reshape(rows // SUB, SUB, width)), axis=0))
-    for i in range(2):
-        sums_ref[i, rows:] = top
-
-
-def exponent(top):
-    return jnp.clip(jnp.ceil(jnp.log2(top)), -100.0, 100.0) - 14.0
+    power = exponent(top)
+    other = sums_ref[1, :rows].reshape(rows // SUB, SUB, width) * jnp.exp2(-power)
+    sums_ref[1, :rows] = other.reshape(rows, width)
+    sums_ref[0, rows:] = top
+    sums_ref[1, rows:] = power
 
 
 def unscaled_sum(got_ref):
@@ -77,12 +80,15 @@
     return total
 
 
-def core_kernel(sums_ref, got_ref, out_ref):
+def core_kernel(me, sums_ref, got_ref, out_ref):
     parts, each, width = out_ref.shape
     each = each - SUB
     rows = parts * each
-    power = exponent(sums_ref[0, rows:] + got_ref[rows:])
-    data = (sums_ref[0, :rows] + got_ref[:rows]).reshape(rows // SUB, SUB, width) * jnp.exp2(-power)
+    got = got_ref[1 - me[0, 0]]
+    theirs = got[rows:]
+    power = exponent(sums_ref[0, rows:] + jnp.exp2(theirs + 14.0))
+    data = sums_ref[0, :rows].reshape(rows // SUB, SUB, width) * jnp.exp2(-power)
+    data = data + got[:rows].reshape(rows // SUB, SUB, width) * jnp.exp2(theirs - power)
     out_ref[:, :each] = data.reshape(parts, each, width)
     out_ref[:, each:] = jnp.broadcast_to(power, (parts, SUB, width))
 
@@ -151,6 +157,7 @@
     rows = oblocks // ncore * probes
     each = rows // nnear
     per = each // probes
+    me = lax.axis_index("core").reshape(1, 1)
     first = (lax.axis_index("core") * nnear + lax.axis_index(NEAR)) * per
     weight = lax.dynamic_slice(obs_weight.reshape(oblocks, 1, width), (first, 0, 0), (per, 1, width))
     sums, jac, bp, bo = pl.pallas_call(
@@ -170,25 +177,27 @@
         ],
         compiler_params=params,
         name="fwd_blocks",
-    )(lax.axis_index("core").reshape(1, 1), block_count, *held)
+    )(me, block_count, *held)
     sums, weight = lax.optimization_barrier((sums, weight))
 
-    def small_call(kernel, shape, dtype, name):
+    def small_call(kernel, shape, dtype, name, in_specs):
         return pl.pallas_call(
             kernel,
             out_shape=jax.ShapeDtypeStruct(shape, dtype),
+            in_specs=in_specs,
             out_specs=vmem,
             compiler_params=little,
             name=name,
         )
 
-    packed = small_call(core_kernel, (nnear, each + SUB, width), jnp.float32, "add_core")(
-        sums, lax.ppermute(sums[1], "core", [(0, 1), (1, 0)])
-    )
+    got = lax.all_gather(sums[1].astype(jnp.float16), "core").astype(jnp.float32)
+    packed = small_call(
+        core_kernel, (nnear, each + SUB, width), jnp.float32, "add_core", [smem, vmem, vmem]
+    )(me, sums, got)
     got = lax.all_to_all(packed.astype(jnp.float16), NEAR, 0, 0, tiled=True).astype(jnp.float32)
-    packed = small_call(near_kernel, (each + SUB, width), jnp.float32, "add_near")(got)
+    packed = small_call(near_kernel, (each + SUB, width), jnp.float32, "add_near", [vmem])(got)
     got = lax.all_gather(packed.astype(jnp.float16), "zh").astype(jnp.float32)
-    scaled = small_call(far_kernel, (nnear, each, width), jnp.bfloat16, "add_far")(got, weight)
+    scaled = small_call(far_kernel, (nnear, each, width), jnp.bfloat16, "add_far", [vmem] * 2)(got, weight)
     scaled = lax.all_to_all(scaled, NEAR, 0, 0, tiled=True).reshape(rows, width)
     scaled = lax.all_gather(scaled, "core", axis=0, tiled=True).reshape(oblocks, probes, width)
 

time: 83.4 us -> 82.3 us (0.987)
  blocking collectives: 66.1 us -> 75.2 us
  starting transfers between devices: 8.79 us -> 0 us
  waiting for transfers between devices: 1.52 us -> 0 us
    ppermute x1 -> x0, starting transfers between devices: 8.79 us -> none  [on_device(): lax.ppermute(sums[1], 'core', [(0, 1), (1, 0)])]
    all_gather x0 -> x1, blocking collectives: none -> 8.69 us  [on_device(): lax.all_gather(sums[1].astype(jnp.float16), 'core').astype(jnp.float32)]
    ppermute x1 -> x0, waiting for transfers between devices: 1.52 us -> none  [on_device(): lax.ppermute(sums[1], 'core', [(0, 1), (1, 0)])]
  transfers between devices with their start and end apart: 1 -> 0, of which waited for: 1 -> 0; matrix products, arithmetic and copies ran while one was open for 0% -> 0% of each run, Pallas kernels for 0% -> 0%
where the time goes in v8:
time: 82.3 us; the launch traced here: 81.7 us
  blocking collectives  75.2 us (91%)
  Pallas kernels  4.79 us (6%)
    all_gather x1, blocking collectives, on_device(): got = lax.all_gather(packed.astype(jnp.float16), 'zh').astype(jnp.float32)  21 us
    all_to_all x1, blocking collectives, on_device(): got = lax.all_to_all(local_terms, GRP, 0, 0, tiled=True)  13.2 us
    all_to_all x1, blocking collectives, on_device(): scaled = lax.all_to_all(scaled, NEAR, 0, 0, tiled=True).reshape(rows, width)  12.8 us
    all_to_all x1, blocking collectives, on_device(): lax.all_to_all(packed.astype(jnp.float16), NEAR, 0, 0, tiled=True)  12.8 us
    all_gather x1, blocking collectives, on_device(): lax.all_gather(sums[1].astype(jnp.float16), 'core').astype(jnp.float32)  8.69 us
    all_gather x1, blocking collectives, on_device(): lax.all_gather(scaled, 'core', axis=0, tiled=True)  6.67 us
    pallas_call x1, Pallas kernels, on_device(): pl.pallas_call(fwd_kernel, out_shape=(jax.ShapeDtypeStruct((ncore, rows +...  3.08 us

profile of v8, /device:TPU:1, one launch (start us, length us, event | category | flops | bytes accessed | tf_op | source)
XLA Modules:
  0.0 81.7 jit_solution(13647577754390702535)
XLA Ops:
  0.0 0.0 copy-start
  0.7 0.1 copy-done
  0.8 3.1 %fwd_blocks.1 = (f32[2,1032,128]{2,1,0:T(8,128)S(1)}, bf16[128,128,128]{2,1,0:T(8,128)(2,1)S(1)}, s32[1,128]{1,0:T(1,128)S(1)}, s32[1,128]{1,0:T(1,128)S(1)}) custom-call(s32[1,1]{1,0:T(1,128)} %bitcast.me, s32[1,1]{1,0:T(1,128)S(6)} %copy.10.cnt, s32[1,128]{1,0:T(1,128)} %bp_hbm.1, s32[1,128]{1,0:T(1,128)} %bo_hbm.1, bf16[32,8192]{1,0:T(8,128)(2,1)} %omega_hbm.1, ...), custom_call_target="tpu_custom_call" | custom-call | tf_op jit(solution)/shard_map/fwd_blocks/pallas_call | solution.py:163
  3.9 8.7 %all_gather.13 = f16[2,1032,128]{2,1,0:T(8,128)(2,1)S(1)} all-gather(f16[1,1032,128]{2,1,0:T(8,128)(2,1)S(1)} %slice_convert_fusion), channel_id=1, replica_groups=mesh['x'=4,'yl'=2,'zh'=4,'zl'=4,'yh'=2,'core'=2] {'core'}, dimensions={0}, use_global_device_ids=true | all-gather | bytes 792576 | tf_op jit(solution)/shard_map/all_gather | solution.py:193
  12.6 0.1 convert_element_type.23.got_ref
  12.7 0.1 add_core.1
  12.8 12.8 %all_to_all.15 = f16[8,136,128]{2,1,0:T(8,128)(2,1)S(1)} all-to-all(f16[8,136,128]{2,1,0:T(8,128)(2,1)S(1)} %convert_element_type.24), channel_id=1, replica_groups=mesh['x'=4,'yl'=2,'zh'=4,'zl'=4,'yh'=2,'core'=2] {'zl','yh'}, dimensions={0} | all-to-all | bytes 557056 | tf_op jit(solution)/shard_map/all_to_all | solution.py:197
  25.6 0.1 add_near.1
  25.7 21.0 %all-gather = f16[544,128]{1,0:T(8,128)(2,1)S(1)} all-gather(f16[136,128]{1,0:T(8,128)(2,1)S(1)} %convert_element_type.26), channel_id=2, replica_groups=mesh['x'=4,'yl'=2,'zh'=4,'zl'=4,'yh'=2,'core'=2] {'zh'}, dimensions={0}, use_global_device_ids=true | all-gather | bytes 174080 | tf_op jit(solution)/shard_map/all_gather | solution.py:199
  46.8 12.8 %all_to_all.16 = bf16[8,128,128]{2,1,0:T(8,128)(2,1)S(1)} all-to-all(bf16[8,128,128]{2,1,0:T(8,128)(2,1)S(1)} %add_far.1), channel_id=1, replica_groups=mesh['x'=4,'yl'=2,'zh'=4,'zl'=4,'yh'=2,'core'=2] {'zl','yh'}, dimensions={0} | all-to-all | bytes 524288 | tf_op jit(solution)/shard_map/all_to_all | solution.py:201
  59.6 6.7 %all_gather.16 = bf16[2048,128]{1,0:T(8,128)(2,1)S(1)} all-gather(bf16[1024,128]{1,0:T(8,128)(2,1)S(1)} %bitcast.17), channel_id=1, replica_groups=mesh['x'=4,'yl'=2,'zh'=4,'zl'=4,'yh'=2,'core'=2] {'core'}, dimensions={0}, use_global_device_ids=true | all-gather | bytes 786432 | tf_op jit(solution)/shard_map/all_gather | solution.py:202
  66.3 1.5 %bwd_blocks.1 = bf16[64,32,128]{2,1,0:T(8,128)(2,1)S(1)} custom-call(s32[1,1]{1,0:T(1,128)S(6)} %copy.10.cnt, s32[1,128]{1,0:T(1,128)S(1)} %get-tuple-element.11.bp, s32[1,128]{1,0:T(1,128)S(1)} %get-tuple-element.12.bo, bf16[64,32,128]{2,1,0:T(8,128)(2,1)S(1)} %bitcast.15, bf16[128,128,128]{2,1,0:T(8,128)(2,1)S(1)} %get-tuple-element.16.jac), custom_call_target="tpu_custom_call" | custom-call | tf_op jit(solution)/shard_map/bwd_blocks/pallas_call | solution.py:204
  67.8 13.2 %all_to_all.17 = bf16[64,32,128]{2,1,0:T(8,128)(2,1)S(1)} all-to-all(bf16[64,32,128]{2,1,0:T(8,128)(2,1)S(1)} %bwd_blocks.1), channel_id=1, replica_groups=mesh['x'=4,'yl'=2,'zh'=4,'zl'=4,'yh'=2,'core'=2] {'x','yl'}, dimensions={0} | all-to-all | bytes 1048576 | tf_op jit(solution)/shard_map/all_to_all | solution.py:215
  81.0 0.1 convert_reduce_fusion
  81.1 0.7 copy_bitcast_fusion
  (7 shorter events, 0.2 us)
Async XLA Ops:
  0.0 0.8 copy-start

commit v9 on v8

--- a/solution.py
+++ b/solution.py
@@ -6,6 +6,7 @@
 from jax.sharding import Mesh, PartitionSpec as P
 
 CHUNK = 64
+GROUP = 4
 SUB = 8
 PAR = ("zh", "zl", "yh", "core")
 NEAR = ("zl", "yh")
@@ -117,20 +118,21 @@
     acc[...] = jnp.zeros_like(acc)
 
     def step(c, carry):
-        for j in range(0, CHUNK, 2):
+        for j in range(0, CHUNK, GROUP):
             first = c * CHUNK + j
-            pair = []
-            for s in (first, first + 1):
+            group = []
+            for s in range(GROUP):
+                s = first + s
                 v = v_ref[bo[0, s]]
-                pair.append(jnp.where(s < n, v, jnp.zeros_like(v)))
-            blocks = jac[pl.ds(first, 2)].reshape(2 * width, width)
+                group.append(jnp.where(s < n, v, jnp.zeros_like(v)))
+            blocks = jac[pl.ds(first, GROUP)].reshape(GROUP * width, width)
             terms = lax.dot_general(
-                jnp.concatenate(pair, axis=0),
+                jnp.concatenate(group, axis=0),
                 blocks,
                 (((1,), (1,)), ((), ())),
                 preferred_element_type=jnp.float32,
             )
-            for i in range(2):
+            for i in range(GROUP):
                 p = bp[0, first + i]
                 acc[p] = acc[p] + terms[i * probes : (i + 1) * probes, i * width : (i + 1) * width]
         return carry
@@ -160,17 +162,17 @@
     me = lax.axis_index("core").reshape(1, 1)
     first = (lax.axis_index("core") * nnear + lax.axis_index(NEAR)) * per
     weight = lax.dynamic_slice(obs_weight.reshape(oblocks, 1, width), (first, 0, 0), (per, 1, width))
-    sums, jac, bp, bo = pl.pallas_call(
+    sums, jac = pl.pallas_call(
         fwd_kernel,
         out_shape=(
             jax.ShapeDtypeStruct((ncore, rows + SUB, width), jnp.float32),
             jax.ShapeDtypeStruct((slots, width, width), jac_blocks.dtype),
-            jax.ShapeDtypeStruct(block_param.shape, jnp.int32),
-            jax.ShapeDtypeStruct(block_obs.shape, jnp.int32),
         ),
         in_specs=[smem] * 2 + [hbm] * 4,
-        out_specs=(vmem, vmem, smem, smem),
+        out_specs=(vmem, vmem),
         scratch_shapes=[
+            pltpu.SMEM(block_param.shape, jnp.int32),
+            pltpu.SMEM(block_obs.shape, jnp.int32),
             pltpu.VMEM(omega.shape, omega.dtype),
             pltpu.SemaphoreType.DMA((3,)),
             pltpu.SemaphoreType.DMA((slots // CHUNK,)),
@@ -209,7 +211,7 @@
         scratch_shapes=[pltpu.VMEM((pblocks, probes, width), jnp.float32)],
         compiler_params=params,
         name="bwd_blocks",
-    )(block_count, bp, bo, scaled, jac)
+    )(block_count, block_param, block_obs, scaled, jac)
 
     n = lax.axis_size(GRP)
     got = lax.all_to_all(local_terms, GRP, 0, 0, tiled=True)

time: 82.3 us -> 81.4 us (0.989)
  no operation moved by 1% of the time
where the time goes in v9:
time: 81.4 us; the launch traced here: 80.4 us
  blocking collectives  74.4 us (91%)
  Pallas kernels  4.12 us (5%)
    all_gather x1, blocking collectives, on_device(): got = lax.all_gather(packed.astype(jnp.float16), 'zh').astype(jnp.float32)  20.7 us
    all_to_all x1, blocking collectives, on_device(): lax.all_to_all(packed.astype(jnp.float16), NEAR, 0, 0, tiled=True)  12.8 us
    all_to_all x1, blocking collectives, on_device(): got = lax.all_to_all(local_terms, GRP, 0, 0, tiled=True)  12.8 us
    all_to_all x1, blocking collectives, on_device(): scaled = lax.all_to_all(scaled, NEAR, 0, 0, tiled=True).reshape(rows, width)  12.6 us
    all_gather x1, blocking collectives, on_device(): lax.all_gather(sums[1].astype(jnp.float16), 'core').astype(jnp.float32)  8.7 us
    all_gather x1, blocking collectives, on_device(): lax.all_gather(scaled, 'core', axis=0, tiled=True)  6.88 us
    pallas_call x1, Pallas kernels, on_device(): pl.pallas_call(fwd_kernel, out_shape=(jax.ShapeDtypeStruct((ncore, rows +...  2.57 us

profile of v9, /device:TPU:1, one launch (start us, length us, event | category | flops | bytes accessed | tf_op | source)
XLA Modules:
  0.0 80.4 jit_solution(3636397300849672398)
XLA Ops:
  0.0 0.0 copy-start
  0.7 0.1 copy-done
  0.8 2.6 %fwd_blocks.1 = (f32[2,1032,128]{2,1,0:T(8,128)S(1)}, bf16[128,128,128]{2,1,0:T(8,128)(2,1)S(1)}) custom-call(s32[1,1]{1,0:T(1,128)} %bitcast.me, s32[1,1]{1,0:T(1,128)S(6)} %copy.10.cnt, s32[1,128]{1,0:T(1,128)} %bp.1, s32[1,128]{1,0:T(1,128)} %bo.1, bf16[32,8192]{1,0:T(8,128)(2,1)} %omega_hbm.1, bf16[1,128,128,128]{3,2,1,0:T(8,128)(2,1)} %jac_hbm.1), custom_call_target="tpu_custom_call" | custom-call | tf_op jit(solution)/shard_map/fwd_blocks/pallas_call | solution.py:165
  3.4 8.7 %all_gather.13 = f16[2,1032,128]{2,1,0:T(8,128)(2,1)S(1)} all-gather(f16[1,1032,128]{2,1,0:T(8,128)(2,1)S(1)} %slice_convert_fusion), channel_id=1, replica_groups=mesh['x'=4,'yl'=2,'zh'=4,'zl'=4,'yh'=2,'core'=2] {'core'}, dimensions={0}, use_global_device_ids=true | all-gather | bytes 792576 | tf_op jit(solution)/shard_map/all_gather | solution.py:195
  12.1 0.1 convert_element_type.23.got_ref
  12.2 0.1 add_core.1
  12.3 12.8 %all_to_all.15 = f16[8,136,128]{2,1,0:T(8,128)(2,1)S(1)} all-to-all(f16[8,136,128]{2,1,0:T(8,128)(2,1)S(1)} %convert_element_type.24), channel_id=1, replica_groups=mesh['x'=4,'yl'=2,'zh'=4,'zl'=4,'yh'=2,'core'=2] {'zl','yh'}, dimensions={0} | all-to-all | bytes 557056 | tf_op jit(solution)/shard_map/all_to_all | solution.py:199
  25.1 0.1 add_near.1
  25.2 20.7 %all-gather = f16[544,128]{1,0:T(8,128)(2,1)S(1)} all-gather(f16[136,128]{1,0:T(8,128)(2,1)S(1)} %convert_element_type.26), channel_id=2, replica_groups=mesh['x'=4,'yl'=2,'zh'=4,'zl'=4,'yh'=2,'core'=2] {'zh'}, dimensions={0}, use_global_device_ids=true | all-gather | bytes 174080 | tf_op jit(solution)/shard_map/all_gather | solution.py:201
  45.9 0.0 copy-start.1
  45.9 0.0 copy-start.2
  46.0 12.6 %all_to_all.16 = bf16[8,128,128]{2,1,0:T(8,128)(2,1)S(1)} all-to-all(bf16[8,128,128]{2,1,0:T(8,128)(2,1)S(1)} %add_far.1), channel_id=1, replica_groups=mesh['x'=4,'yl'=2,'zh'=4,'zl'=4,'yh'=2,'core'=2] {'zl','yh'}, dimensions={0} | all-to-all | bytes 524288 | tf_op jit(solution)/shard_map/all_to_all | solution.py:203
  58.6 6.9 %all_gather.16 = bf16[2048,128]{1,0:T(8,128)(2,1)S(1)} all-gather(bf16[1024,128]{1,0:T(8,128)(2,1)S(1)} %bitcast.17), channel_id=1, replica_groups=mesh['x'=4,'yl'=2,'zh'=4,'zl'=4,'yh'=2,'core'=2] {'core'}, dimensions={0}, use_global_device_ids=true | all-gather | bytes 786432 | tf_op jit(solution)/shard_map/all_gather | solution.py:204
  65.5 0.0 copy-done.1
  65.5 0.0 copy-done.2
  65.5 1.4 %bwd_blocks.1 = bf16[64,32,128]{2,1,0:T(8,128)(2,1)S(1)} custom-call(s32[1,1]{1,0:T(1,128)S(6)} %copy.10.cnt, s32[1,128]{1,0:T(1,128)S(1)} %copy-done.1, s32[1,128]{1,0:T(1,128)S(1)} %copy-done.2, bf16[64,32,128]{2,1,0:T(8,128)(2,1)S(1)} %bitcast.15, bf16[128,128,128]{2,1,0:T(8,128)(2,1)S(1)} %get-tuple-element.12.jac), custom_call_target="tpu_custom_call" | custom-call | tf_op jit(solution)/shard_map/bwd_blocks/pallas_call | solution.py:206
  66.9 12.8 %all_to_all.17 = bf16[64,32,128]{2,1,0:T(8,128)(2,1)S(1)} all-to-all(bf16[64,32,128]{2,1,0:T(8,128)(2,1)S(1)} %bwd_blocks.1), channel_id=1, replica_groups=mesh['x'=4,'yl'=2,'zh'=4,'zl'=4,'yh'=2,'core'=2] {'x','yl'}, dimensions={0} | all-to-all | bytes 1048576 | tf_op jit(solution)/shard_map/all_to_all | solution.py:217
  79.7 0.1 convert_reduce_fusion
  79.7 0.7 copy_bitcast_fusion
  (7 shorter events, 0.2 us)
Async XLA Ops:
  0.0 0.8 copy-start
  45.9 19.6 %copy-start.1 = (s32[1,128]{1,0:T(1,128)S(1)}, s32[1,128]{1,0:T(1,128)}, u32[]{:S(2)}) copy-start(s32[1,128]{1,0:T(1,128)} %bp.1) | copy-start | bytes 1540
  45.9 19.6 %copy-start.2 = (s32[1,128]{1,0:T(1,128)S(1)}, s32[1,128]{1,0:T(1,128)}, u32[]{:S(2)}) copy-start(s32[1,128]{1,0:T(1,128)} %bo.1) | copy-start | bytes 1540

commit v10 on v9

--- a/solution.py
+++ b/solution.py
@@ -109,6 +109,15 @@
     total = unscaled_sum(got_ref).reshape(per, rows // per, width)
     scaled = (total * weight_ref[...]).reshape(rows, width).astype(out_ref.dtype)
     out_ref[...] = jnp.broadcast_to(scaled, (copies, rows, width))
+
+
+def total_kernel(got_ref, out_ref):
+    parts, blocks, _, width = got_ref.shape
+    for j in range(blocks):
+        total = got_ref[0, j].astype(jnp.float32)
+        for i in range(1, parts):
+            total = total + got_ref[i, j].astype(jnp.float32)
+        out_ref[:, j * width : (j + 1) * width] = total
 
 
 def bwd_kernel(cnt, bp, bo, v_ref, jac, out_ref, acc):
@@ -215,9 +224,10 @@
 
     n = lax.axis_size(GRP)
     got = lax.all_to_all(local_terms, GRP, 0, 0, tiled=True)
-    got = got.reshape(n, pblocks // n, probes, width).astype(jnp.float32)
-    total = jnp.sum(got, axis=0)
-    return jnp.transpose(total, (1, 0, 2)).reshape(probes, pblocks // n * width)
+    got = got.reshape(n, pblocks // n, probes, width)
+    return small_call(
+        total_kernel, (probes, pblocks // n * width), jnp.float32, "add_groups", [vmem]
+    )(got)
 
 
 def solution(mesh):

time: 81.4 us -> 81.8 us (level)
  Pallas kernels: 4.12 us -> 6.33 us
where the time goes in v10:
time: 81.8 us; the launch traced here: 81.2 us
  blocking collectives  73.8 us (90%)
  Pallas kernels  6.33 us (8%)
    all_gather x1, blocking collectives, on_device(): got = lax.all_gather(packed.astype(jnp.float16), 'zh').astype(jnp.float32)  20.7 us
    all_to_all x1, blocking collectives, on_device(): got = lax.all_to_all(local_terms, GRP, 0, 0, tiled=True)  12.9 us
    all_to_all x1, blocking collectives, on_device(): lax.all_to_all(packed.astype(jnp.float16), NEAR, 0, 0, tiled=True)  12.8 us
    all_to_all x1, blocking collectives, on_device(): scaled = lax.all_to_all(scaled, NEAR, 0, 0, tiled=True).reshape(rows, width)  12.6 us
    all_gather x1, blocking collectives, on_device(): lax.all_gather(sums[1].astype(jnp.float16), 'core').astype(jnp.float32)  7.94 us
    all_gather x1, blocking collectives, on_device(): lax.all_gather(scaled, 'core', axis=0, tiled=True)  6.89 us
    pallas_call x1, Pallas kernels, on_device(): pl.pallas_call(fwd_kernel, out_shape=(jax.ShapeDtypeStruct((ncore, rows +...  3.33 us
    pallas_call x1, Pallas kernels, on_device(): pl.pallas_call(bwd_kernel, out_shape=jax.ShapeDtypeStruct((pblocks, probe...  2.1 us

profile of v10, /device:TPU:1, one launch (start us, length us, event | category | flops | bytes accessed | tf_op | source)
XLA Modules:
  0.0 81.2 jit_solution(8587669834813192985)
XLA Ops:
  0.0 0.0 copy-start
  0.7 0.1 copy-done
  0.8 3.3 %fwd_blocks.1 = (f32[2,1032,128]{2,1,0:T(8,128)S(1)}, bf16[128,128,128]{2,1,0:T(8,128)(2,1)S(1)}) custom-call(s32[1,1]{1,0:T(1,128)} %bitcast.me, s32[1,1]{1,0:T(1,128)S(6)} %copy.7.cnt, s32[1,128]{1,0:T(1,128)} %bp.1, s32[1,128]{1,0:T(1,128)} %bo.1, bf16[32,8192]{1,0:T(8,128)(2,1)} %omega_hbm.1, bf16[1,128,128,128]{3,2,1,0:T(8,128)(2,1)} %jac_hbm.1), custom_call_target="tpu_custom_call" | custom-call | tf_op jit(solution)/shard_map/fwd_blocks/pallas_call | solution.py:174
  4.2 7.9 %all_gather.13 = f16[2,1032,128]{2,1,0:T(8,128)(2,1)S(1)} all-gather(f16[1,1032,128]{2,1,0:T(8,128)(2,1)S(1)} %slice_convert_fusion), channel_id=1, replica_groups=mesh['x'=4,'yl'=2,'zh'=4,'zl'=4,'yh'=2,'core'=2] {'core'}, dimensions={0}, use_global_device_ids=true | all-gather | bytes 792576 | tf_op jit(solution)/shard_map/all_gather | solution.py:204
  12.1 0.1 convert_element_type.17.got_ref
  12.2 0.1 add_core.1
  12.3 12.8 %all_to_all.15 = f16[8,136,128]{2,1,0:T(8,128)(2,1)S(1)} all-to-all(f16[8,136,128]{2,1,0:T(8,128)(2,1)S(1)} %convert_element_type.18), channel_id=1, replica_groups=mesh['x'=4,'yl'=2,'zh'=4,'zl'=4,'yh'=2,'core'=2] {'zl','yh'}, dimensions={0} | all-to-all | bytes 557056 | tf_op jit(solution)/shard_map/all_to_all | solution.py:208
  25.1 0.1 add_near.1
  25.2 20.7 %all-gather = f16[544,128]{1,0:T(8,128)(2,1)S(1)} all-gather(f16[136,128]{1,0:T(8,128)(2,1)S(1)} %convert_element_type.20), channel_id=2, replica_groups=mesh['x'=4,'yl'=2,'zh'=4,'zl'=4,'yh'=2,'core'=2] {'zh'}, dimensions={0}, use_global_device_ids=true | all-gather | bytes 174080 | tf_op jit(solution)/shard_map/all_gather | solution.py:210
  45.9 0.0 copy-start.1
  45.9 0.0 copy-start.2
  46.0 12.6 %all_to_all.16 = bf16[8,128,128]{2,1,0:T(8,128)(2,1)S(1)} all-to-all(bf16[8,128,128]{2,1,0:T(8,128)(2,1)S(1)} %add_far.1), channel_id=1, replica_groups=mesh['x'=4,'yl'=2,'zh'=4,'zl'=4,'yh'=2,'core'=2] {'zl','yh'}, dimensions={0} | all-to-all | bytes 524288 | tf_op jit(solution)/shard_map/all_to_all | solution.py:212
  58.6 6.9 %all_gather.16 = bf16[2048,128]{1,0:T(8,128)(2,1)S(1)} all-gather(bf16[1024,128]{1,0:T(8,128)(2,1)S(1)} %bitcast.10), channel_id=1, replica_groups=mesh['x'=4,'yl'=2,'zh'=4,'zl'=4,'yh'=2,'core'=2] {'core'}, dimensions={0}, use_global_device_ids=true | all-gather | bytes 786432 | tf_op jit(solution)/shard_map/all_gather | solution.py:213
  65.5 0.0 copy-done.1
  65.5 0.0 copy-done.2
  65.5 2.1 %bwd_blocks.1 = bf16[64,32,128]{2,1,0:T(8,128)(2,1)S(1)} custom-call(s32[1,1]{1,0:T(1,128)S(6)} %copy.7.cnt, s32[1,128]{1,0:T(1,128)S(1)} %copy-done.1, s32[1,128]{1,0:T(1,128)S(1)} %copy-done.2, bf16[64,32,128]{2,1,0:T(8,128)(2,1)S(1)} %bitcast.8, bf16[128,128,128]{2,1,0:T(8,128)(2,1)S(1)} %get-tuple-element.12.jac), custom_call_target="tpu_custom_call" | custom-call | tf_op jit(solution)/shard_map/bwd_blocks/pallas_call | solution.py:215
  67.6 12.9 %all_to_all.17 = bf16[64,32,128]{2,1,0:T(8,128)(2,1)S(1)} all-to-all(bf16[64,32,128]{2,1,0:T(8,128)(2,1)S(1)} %bwd_blocks.1), channel_id=1, replica_groups=mesh['x'=4,'yl'=2,'zh'=4,'zl'=4,'yh'=2,'core'=2] {'x','yl'}, dimensions={0} | all-to-all | bytes 1048576 | tf_op jit(solution)/shard_map/all_to_all | solution.py:226
  80.5 0.7 add_groups.1
  (7 shorter events, 0.2 us)
Async XLA Ops:
  0.0 0.8 copy-start
  45.9 19.6 %copy-start.1 = (s32[1,128]{1,0:T(1,128)S(1)}, s32[1,128]{1,0:T(1,128)}, u32[]{:S(2)}) copy-start(s32[1,128]{1,0:T(1,128)} %bp.1) | copy-start | bytes 1540
  45.9 19.6 %copy-start.2 = (s32[1,128]{1,0:T(1,128)S(1)}, s32[1,128]{1,0:T(1,128)}, u32[]{:S(2)}) copy-start(s32[1,128]{1,0:T(1,128)} %bo.1) | copy-start | bytes 1540

commit v11 on v10

--- a/solution.py
+++ b/solution.py
@@ -6,6 +6,7 @@
 from jax.sharding import Mesh, PartitionSpec as P
 
 CHUNK = 64
+PIECES = ((0, 64), (64, 32), (96, 32))
 GROUP = 4
 SUB = 8
 PAR = ("zh", "zl", "yh", "core")
@@ -32,25 +33,25 @@
         copy.start()
     n = cnt[0, 0]
 
-    def chunk(c):
-        at = pl.ds(pl.multiple_of(c * CHUNK, CHUNK), CHUNK)
-        return pltpu.make_async_copy(jac_hbm.at[0, at], jac.at[at], jsems.at[c])
-
-    for c in range(jac.shape[0] // CHUNK):
-
-        @pl.when(c * CHUNK < n)
-        def _():
-            chunk(c).start()
+    def piece(i):
+        at = pl.ds(*PIECES[i])
+        return pltpu.make_async_copy(jac_hbm.at[0, at], jac.at[at], jsems.at[i])
+
+    piece(0).start()
+
+    @pl.when(n > CHUNK)
+    def _():
+        for i in range(1, len(PIECES)):
+            piece(i).start()
 
     sums_ref[...] = jnp.zeros_like(sums_ref)
     flip = me[0, 0] * half
     for copy in small:
         copy.wait()
 
-    def step(c, carry):
-        chunk(c).wait()
-        for j in range(CHUNK):
-            s = c * CHUNK + j
+    def use(i):
+        piece(i).wait()
+        for s in range(PIECES[i][0], sum(PIECES[i])):
             at = pl.multiple_of(bp[0, s] * width, width)
             panel = omega[:, pl.ds(at, width)]
             panel = jnp.where(s < n, panel, jnp.zeros_like(panel))
@@ -58,9 +59,14 @@
             o = bo[0, s] ^ flip
             at = pl.ds(pl.multiple_of(o % half * probes, probes), probes)
             sums_ref[o // half, at] = sums_ref[o // half, at] + term
-        return carry
-
-    lax.fori_loop(0, (n + CHUNK - 1) // CHUNK, step, 0)
+
+    use(0)
+
+    @pl.when(n > CHUNK)
+    def _():
+        for i in range(1, len(PIECES)):
+            use(i)
+
     top = jnp.zeros((SUB, width), jnp.float32)
     for i in range(2):
         top = jnp.maximum(top, jnp.max(jnp.abs(sums_ref[i, :rows].reshape(rows // SUB, SUB, width)), axis=0))
@@ -184,7 +190,7 @@
             pltpu.SMEM(block_obs.shape, jnp.int32),
             pltpu.VMEM(omega.shape, omega.dtype),
             pltpu.SemaphoreType.DMA((3,)),
-            pltpu.SemaphoreType.DMA((slots // CHUNK,)),
+            pltpu.SemaphoreType.DMA((len(PIECES),)),
         ],
         compiler_params=params,
         name="fwd_blocks",

time: 81.8 us -> 81.5 us (level)
  Pallas kernels: 6.33 us -> 4.78 us
  blocking collectives: 73.8 us -> 75.1 us
    pallas_call x1, Pallas kernels: 3.33 us -> 2.5 us  [on_device(): pl.pallas_call(fwd_kernel, out_shape=(jax.ShapeDtypeStruct((ncore, rows +...]
where the time goes in v11:
time: 81.5 us; the launch traced here: 81 us
  blocking collectives  75.1 us (92%)
  Pallas kernels  4.78 us (6%)
    all_gather x1, blocking collectives, on_device(): got = lax.all_gather(packed.astype(jnp.float16), 'zh').astype(jnp.float32)  20.7 us
    all_to_all x1, blocking collectives, on_device(): got = lax.all_to_all(local_terms, GRP, 0, 0, tiled=True)  13.4 us
    all_to_all x1, blocking collectives, on_device(): lax.all_to_all(packed.astype(jnp.float16), NEAR, 0, 0, tiled=True)  12.8 us
    all_to_all x1, blocking collectives, on_device(): scaled = lax.all_to_all(scaled, NEAR, 0, 0, tiled=True).reshape(rows, width)  12.6 us
    all_gather x1, blocking collectives, on_device(): lax.all_gather(sums[1].astype(jnp.float16), 'core').astype(jnp.float32)  8.69 us
    all_gather x1, blocking collectives, on_device(): lax.all_gather(scaled, 'core', axis=0, tiled=True)  6.88 us
    pallas_call x1, Pallas kernels, on_device(): pl.pallas_call(fwd_kernel, out_shape=(jax.ShapeDtypeStruct((ncore, rows +...  2.5 us

profile of v11, /device:TPU:1, one launch (start us, length us, event | category | flops | bytes accessed | tf_op | source)
XLA Modules:
  0.0 81.0 jit_solution(10850205915752265241)
XLA Ops:
  0.0 0.0 copy-start
  0.7 0.1 copy-done
  0.8 2.5 %fwd_blocks.1 = (f32[2,1032,128]{2,1,0:T(8,128)S(1)}, bf16[128,128,128]{2,1,0:T(8,128)(2,1)S(1)}) custom-call(s32[1,1]{1,0:T(1,128)} %bitcast.me, s32[1,1]{1,0:T(1,128)S(6)} %copy.7.cnt, s32[1,128]{1,0:T(1,128)} %bp.1, s32[1,128]{1,0:T(1,128)} %bo.1, bf16[32,8192]{1,0:T(8,128)(2,1)} %omega_hbm.1, bf16[1,128,128,128]{3,2,1,0:T(8,128)(2,1)} %jac_hbm.1), custom_call_target="tpu_custom_call" | custom-call | tf_op jit(solution)/shard_map/fwd_blocks/pallas_call | solution.py:180
  3.3 8.7 %all_gather.13 = f16[2,1032,128]{2,1,0:T(8,128)(2,1)S(1)} all-gather(f16[1,1032,128]{2,1,0:T(8,128)(2,1)S(1)} %slice_convert_fusion), channel_id=1, replica_groups=mesh['x'=4,'yl'=2,'zh'=4,'zl'=4,'yh'=2,'core'=2] {'core'}, dimensions={0}, use_global_device_ids=true | all-gather | bytes 792576 | tf_op jit(solution)/shard_map/all_gather | solution.py:210
  12.0 0.1 convert_element_type.17.got_ref
  12.1 0.1 add_core.1
  12.2 12.8 %all_to_all.15 = f16[8,136,128]{2,1,0:T(8,128)(2,1)S(1)} all-to-all(f16[8,136,128]{2,1,0:T(8,128)(2,1)S(1)} %convert_element_type.18), channel_id=1, replica_groups=mesh['x'=4,'yl'=2,'zh'=4,'zl'=4,'yh'=2,'core'=2] {'zl','yh'}, dimensions={0} | all-to-all | bytes 557056 | tf_op jit(solution)/shard_map/all_to_all | solution.py:214
  25.1 0.1 add_near.1
  25.2 20.7 %all-gather = f16[544,128]{1,0:T(8,128)(2,1)S(1)} all-gather(f16[136,128]{1,0:T(8,128)(2,1)S(1)} %convert_element_type.20), channel_id=2, replica_groups=mesh['x'=4,'yl'=2,'zh'=4,'zl'=4,'yh'=2,'core'=2] {'zh'}, dimensions={0}, use_global_device_ids=true | all-gather | bytes 174080 | tf_op jit(solution)/shard_map/all_gather | solution.py:216
  45.9 0.0 copy-start.1
  45.9 0.0 copy-start.2
  45.9 12.6 %all_to_all.16 = bf16[8,128,128]{2,1,0:T(8,128)(2,1)S(1)} all-to-all(bf16[8,128,128]{2,1,0:T(8,128)(2,1)S(1)} %add_far.1), channel_id=1, replica_groups=mesh['x'=4,'yl'=2,'zh'=4,'zl'=4,'yh'=2,'core'=2] {'zl','yh'}, dimensions={0} | all-to-all | bytes 524288 | tf_op jit(solution)/shard_map/all_to_all | solution.py:218
  58.6 6.9 %all_gather.16 = bf16[2048,128]{1,0:T(8,128)(2,1)S(1)} all-gather(bf16[1024,128]{1,0:T(8,128)(2,1)S(1)} %bitcast.10), channel_id=1, replica_groups=mesh['x'=4,'yl'=2,'zh'=4,'zl'=4,'yh'=2,'core'=2] {'core'}, dimensions={0}, use_global_device_ids=true | all-gather | bytes 786432 | tf_op jit(solution)/shard_map/all_gather | solution.py:219
  65.4 0.0 copy-done.1
  65.4 0.0 copy-done.2
  65.4 1.4 %bwd_blocks.1 = bf16[64,32,128]{2,1,0:T(8,128)(2,1)S(1)} custom-call(s32[1,1]{1,0:T(1,128)S(6)} %copy.7.cnt, s32[1,128]{1,0:T(1,128)S(1)} %copy-done.1, s32[1,128]{1,0:T(1,128)S(1)} %copy-done.2, bf16[64,32,128]{2,1,0:T(8,128)(2,1)S(1)} %bitcast.8, bf16[128,128,128]{2,1,0:T(8,128)(2,1)S(1)} %get-tuple-element.12.jac), custom_call_target="tpu_custom_call" | custom-call | tf_op jit(solution)/shard_map/bwd_blocks/pallas_call | solution.py:221
  66.8 13.4 %all_to_all.17 = bf16[64,32,128]{2,1,0:T(8,128)(2,1)S(1)} all-to-all(bf16[64,32,128]{2,1,0:T(8,128)(2,1)S(1)} %bwd_blocks.1), channel_id=1, replica_groups=mesh['x'=4,'yl'=2,'zh'=4,'zl'=4,'yh'=2,'core'=2] {'x','yl'}, dimensions={0} | all-to-all | bytes 1048576 | tf_op jit(solution)/shard_map/all_to_all | solution.py:232
  80.3 0.7 add_groups.1
  (7 shorter events, 0.2 us)
Async XLA Ops:
  0.0 0.8 copy-start
  45.9 19.6 %copy-start.1 = (s32[1,128]{1,0:T(1,128)S(1)}, s32[1,128]{1,0:T(1,128)}, u32[]{:S(2)}) copy-start(s32[1,128]{1,0:T(1,128)} %bp.1) | copy-start | bytes 1540
  45.9 19.6 %copy-start.2 = (s32[1,128]{1,0:T(1,128)S(1)}, s32[1,128]{1,0:T(1,128)}, u32[]{:S(2)}) copy-start(s32[1,128]{1,0:T(1,128)} %bo.1) | copy-start | bytes 1540

commit v12 on v10

--- a/solution.py
+++ b/solution.py
@@ -28,8 +28,6 @@
         pltpu.make_async_copy(src, dst, sems.at[i])
         for i, (src, dst) in enumerate(((bp_hbm, bp), (bo_hbm, bo), (omega_hbm, omega)))
     ]
-    for copy in small:
-        copy.start()
     n = cnt[0, 0]
 
     def chunk(c):
@@ -42,6 +40,8 @@
         def _():
             chunk(c).start()
 
+    for copy in small:
+        copy.start()
     sums_ref[...] = jnp.zeros_like(sums_ref)
     flip = me[0, 0] * half
     for copy in small:

time: 81.8 us -> 81.9 us (level)
  blocking collectives: 73.8 us -> 75.5 us
  Pallas kernels: 6.33 us -> 4.85 us
    all_gather x1, blocking collectives: 20.7 us -> 19.4 us  [on_device(): got = lax.all_gather(packed.astype(jnp.float16), 'zh').astype(jnp.float32)]
    all_to_all x1, blocking collectives: 12.8 us -> 14.1 us  [on_device(): lax.all_to_all(packed.astype(jnp.float16), NEAR, 0, 0, tiled=True)]
    all_to_all x1, blocking collectives: 12.9 us -> 13.8 us  [on_device(): got = lax.all_to_all(local_terms, GRP, 0, 0, tiled=True)]
where the time goes in v12:
time: 81.9 us; the launch traced here: 81.4 us
  blocking collectives  75.5 us (92%)
  Pallas kernels  4.85 us (6%)
    all_gather x1, blocking collectives, on_device(): got = lax.all_gather(packed.astype(jnp.float16), 'zh').astype(jnp.float32)  19.4 us
    all_to_all x1, blocking collectives, on_device(): lax.all_to_all(packed.astype(jnp.float16), NEAR, 0, 0, tiled=True)  14.1 us
    all_to_all x1, blocking collectives, on_device(): got = lax.all_to_all(local_terms, GRP, 0, 0, tiled=True)  13.8 us
    all_to_all x1, blocking collectives, on_device(): scaled = lax.all_to_all(scaled, NEAR, 0, 0, tiled=True).reshape(rows, width)  12.6 us
    all_gather x1, blocking collectives, on_device(): lax.all_gather(sums[1].astype(jnp.float16), 'core').astype(jnp.float32)  8.69 us
    all_gather x1, blocking collectives, on_device(): lax.all_gather(scaled, 'core', axis=0, tiled=True)  6.87 us
    pallas_call x1, Pallas kernels, on_device(): pl.pallas_call(fwd_kernel, out_shape=(jax.ShapeDtypeStruct((ncore, rows +...  2.58 us

profile of v12, /device:TPU:1, one launch (start us, length us, event | category | flops | bytes accessed | tf_op | source)
XLA Modules:
  0.0 81.4 jit_solution(16809004560558483313)
XLA Ops:
  0.0 0.0 copy-start
  0.7 0.1 copy-done
  0.8 2.6 %fwd_blocks.1 = (f32[2,1032,128]{2,1,0:T(8,128)S(1)}, bf16[128,128,128]{2,1,0:T(8,128)(2,1)S(1)}) custom-call(s32[1,1]{1,0:T(1,128)} %bitcast.me, s32[1,1]{1,0:T(1,128)S(6)} %copy.7.cnt, s32[1,128]{1,0:T(1,128)} %bp.1, s32[1,128]{1,0:T(1,128)} %bo.1, bf16[32,8192]{1,0:T(8,128)(2,1)} %omega_hbm.1, bf16[1,128,128,128]{3,2,1,0:T(8,128)(2,1)} %jac_hbm.1), custom_call_target="tpu_custom_call" | custom-call | tf_op jit(solution)/shard_map/fwd_blocks/pallas_call | solution.py:174
  3.4 8.7 %all_gather.13 = f16[2,1032,128]{2,1,0:T(8,128)(2,1)S(1)} all-gather(f16[1,1032,128]{2,1,0:T(8,128)(2,1)S(1)} %slice_convert_fusion), channel_id=1, replica_groups=mesh['x'=4,'yl'=2,'zh'=4,'zl'=4,'yh'=2,'core'=2] {'core'}, dimensions={0}, use_global_device_ids=true | all-gather | bytes 792576 | tf_op jit(solution)/shard_map/all_gather | solution.py:204
  12.1 0.1 convert_element_type.17.got_ref
  12.2 0.1 add_core.1
  12.3 14.1 %all_to_all.15 = f16[8,136,128]{2,1,0:T(8,128)(2,1)S(1)} all-to-all(f16[8,136,128]{2,1,0:T(8,128)(2,1)S(1)} %convert_element_type.18), channel_id=1, replica_groups=mesh['x'=4,'yl'=2,'zh'=4,'zl'=4,'yh'=2,'core'=2] {'zl','yh'}, dimensions={0} | all-to-all | bytes 557056 | tf_op jit(solution)/shard_map/all_to_all | solution.py:208
  26.5 0.1 add_near.1
  26.6 19.4 %all-gather = f16[544,128]{1,0:T(8,128)(2,1)S(1)} all-gather(f16[136,128]{1,0:T(8,128)(2,1)S(1)} %convert_element_type.20), channel_id=2, replica_groups=mesh['x'=4,'yl'=2,'zh'=4,'zl'=4,'yh'=2,'core'=2] {'zh'}, dimensions={0}, use_global_device_ids=true | all-gather | bytes 174080 | tf_op jit(solution)/shard_map/all_gather | solution.py:210
  45.9 0.0 copy-start.1
  45.9 0.0 copy-start.2
  46.0 12.6 %all_to_all.16 = bf16[8,128,128]{2,1,0:T(8,128)(2,1)S(1)} all-to-all(bf16[8,128,128]{2,1,0:T(8,128)(2,1)S(1)} %add_far.1), channel_id=1, replica_groups=mesh['x'=4,'yl'=2,'zh'=4,'zl'=4,'yh'=2,'core'=2] {'zl','yh'}, dimensions={0} | all-to-all | bytes 524288 | tf_op jit(solution)/shard_map/all_to_all | solution.py:212
  58.6 6.9 %all_gather.16 = bf16[2048,128]{1,0:T(8,128)(2,1)S(1)} all-gather(bf16[1024,128]{1,0:T(8,128)(2,1)S(1)} %bitcast.10), channel_id=1, replica_groups=mesh['x'=4,'yl'=2,'zh'=4,'zl'=4,'yh'=2,'core'=2] {'core'}, dimensions={0}, use_global_device_ids=true | all-gather | bytes 786432 | tf_op jit(solution)/shard_map/all_gather | solution.py:213
  65.5 0.0 copy-done.1
  65.5 0.0 copy-done.2
  65.5 1.4 %bwd_blocks.1 = bf16[64,32,128]{2,1,0:T(8,128)(2,1)S(1)} custom-call(s32[1,1]{1,0:T(1,128)S(6)} %copy.7.cnt, s32[1,128]{1,0:T(1,128)S(1)} %copy-done.1, s32[1,128]{1,0:T(1,128)S(1)} %copy-done.2, bf16[64,32,128]{2,1,0:T(8,128)(2,1)S(1)} %bitcast.8, bf16[128,128,128]{2,1,0:T(8,128)(2,1)S(1)} %get-tuple-element.12.jac), custom_call_target="tpu_custom_call" | custom-call | tf_op jit(solution)/shard_map/bwd_blocks/pallas_call | solution.py:215
  66.9 13.8 %all_to_all.17 = bf16[64,32,128]{2,1,0:T(8,128)(2,1)S(1)} all-to-all(bf16[64,32,128]{2,1,0:T(8,128)(2,1)S(1)} %bwd_blocks.1), channel_id=1, replica_groups=mesh['x'=4,'yl'=2,'zh'=4,'zl'=4,'yh'=2,'core'=2] {'x','yl'}, dimensions={0} | all-to-all | bytes 1048576 | tf_op jit(solution)/shard_map/all_to_all | solution.py:226
  80.7 0.7 add_groups.1
  (7 shorter events, 0.2 us)
Async XLA Ops:
  0.0 0.8 copy-start
  45.9 19.6 %copy-start.1 = (s32[1,128]{1,0:T(1,128)S(1)}, s32[1,128]{1,0:T(1,128)}, u32[]{:S(2)}) copy-start(s32[1,128]{1,0:T(1,128)} %bp.1) | copy-start | bytes 1540
  45.9 19.6 %copy-start.2 = (s32[1,128]{1,0:T(1,128)S(1)}, s32[1,128]{1,0:T(1,128)}, u32[]{:S(2)}) copy-start(s32[1,128]{1,0:T(1,128)} %bo.1) | copy-start | bytes 1540
